TPU v7x, 32 devices: a whole 2x2x4 slice. The times are simulated.
32 devices in a mesh: ctx: 4 (over y, x), fsdp: 8 (over z, core).
Axes of the slice: x: 2, y: 2, z: 4, core: 2. Of those that a mesh axis runs over, the one named last changes fastest.
Arguments:
- tokens: bfloat16 [8, 1024, 2048], P('fsdp', 'ctx'), may hold values from -6 to 6
- seq_ids: int32 [8, 1024], P('fsdp', 'ctx'), may hold values from 0 to 1, as said below
- positions: int32 [8, 1024], P('fsdp', 'ctx'), may hold values from 0 to 767, as said below
- ln1_gain: bfloat16 [2048], replicated, may hold values from 0.5 to 1.5
- ln1_bias: bfloat16 [2048], replicated, may hold values from -3 to 3
- ln2_gain: bfloat16 [2048], replicated, may hold values from 0.5 to 1.5
- ln2_bias: bfloat16 [2048], replicated, may hold values from -3 to 3
- w_qkv: bfloat16 [2048, 6144], P(('ctx', 'fsdp'))
- w_out: bfloat16 [2048, 2048], P(('ctx', 'fsdp')), may hold values from -2 to 2
- w_up: bfloat16 [2048, 8192], P(('ctx', 'fsdp')), may hold values from -0.125 to 0.125
- w_down: bfloat16 [2048, 8192], P(('ctx', 'fsdp')), may hold values from -0.0625 to 0.0625
- grad_out: bfloat16 [8, 1024, 2048], P('fsdp', 'ctx'), may hold values from -6 to 6
Outputs:
- output: bfloat16 [8, 1024, 2048], P('fsdp', 'ctx')
- grad_tokens: bfloat16 [8, 1024, 2048], P('fsdp', 'ctx')
- grad_ln1_gain: float32 [2048], P(('ctx', 'fsdp'))
- grad_ln1_bias: float32 [2048], P(('ctx', 'fsdp'))
- grad_ln2_gain: float32 [2048], P(('ctx', 'fsdp'))
- grad_ln2_bias: float32 [2048], P(('ctx', 'fsdp'))
- grad_w_qkv: float32 [2048, 6144], P(('ctx', 'fsdp'))
- grad_w_out: float32 [2048, 2048], P(('ctx', 'fsdp'))
- grad_w_up: float32 [2048, 8192], P(('ctx', 'fsdp'))
- grad_w_down: float32 [2048, 8192], P(('ctx', 'fsdp'))
Inputs may be any that keep to these rules, and one draw needn't show every extreme that they name: `seq_ids`: in each pack the tokens of document 0 come first and those of document 1 follow; each document has 256 tokens or more. `positions`: A token's index within its document, 0 at the document's first token.
All inputs are finite; a program needn't handle non-finite values.
Results may differ from a plain program's by a relative error of at most 0.03.
Values may be sent and summed in bfloat16 or wider, within the bound.
No kernel may reach another device: no remote copies, remote signals or barrier semaphores. Data moves between devices by JAX's collectives and lax.ppermute only.
A program may use at most 768 MiB of HBM per device.

v0:
```python
import jax
import jax.numpy as jnp
import numpy as np
from jax import lax
from jax.sharding import Mesh
from jax.sharding import PartitionSpec as P

HEADS = 8
HEAD_DIM = 256
ROT = 64


NORM_EPS = 1e-05
NEG_FILL = -1e30
ROPE_BASE = 10000.0
CORES = 2
FSDP = ("line", "core")
ROWS_FIRST = (((0,), (0,)), ((), ()))
COLS_BOTH = (((1,), (1,)), ((), ()))


def swap(value, step):
    count = lax.axis_size("ctx")
    return lax.ppermute(value, "ctx", [(i, i ^ step) for i in range(count)])


def gather_ctx(block):
    count = lax.axis_size("ctx")
    return jnp.concatenate([block] + [swap(block, k) for k in range(1, count)], 0)


def scatter_ctx(parts, rows):
    count = lax.axis_size("ctx")
    low = parts.astype(jnp.bfloat16)
    total = parts[:rows]
    for k in range(1, count):
        total = total + swap(low[k * rows : (k + 1) * rows], k).astype(jnp.float32)
    return total


def turn(value, first, second):
    lead, width = value.shape[:-1], value.shape[-1]
    split = value.reshape(*lead, first, second, width // (first * second))
    return jnp.swapaxes(split, -3, -2).reshape(*lead, width)


def normalize(inputs):
    row_mean = jnp.mean(inputs, axis=-1, keepdims=True)
    centred = inputs - row_mean
    inv_std = lax.rsqrt(jnp.mean(centred * centred, axis=-1, keepdims=True) + NORM_EPS)
    return (centred * inv_std, inv_std)


def rotary_tables(position_row):
    half_dims = ROT // 2
    freqs = ROPE_BASE ** (-(jnp.arange(half_dims, dtype=jnp.float32) * 2.0) / ROT)
    angles = position_row.astype(jnp.float32)[:, None] * freqs[None, :]
    cosines = jnp.cos(angles)
    sines = jnp.sin(angles)
    return (
        jnp.concatenate([cosines, cosines], -1)[:, None, :],
        jnp.concatenate([sines, sines], -1)[:, None, :],
    )


def rotate(heads, cosines, sines):
    half_dims = ROT // 2
    turned = heads[..., :ROT]
    swapped = jnp.concatenate([-turned[..., half_dims:], turned[..., :half_dims]], -1)
    return jnp.concatenate([turned * cosines + swapped * sines, heads[..., ROT:]], -1)


def after(value, earlier):
    return value if earlier is None else lax.optimization_barrier((value, earlier))[0]


def exchange_columns(shard, groups, earlier=None):
    count = lax.axis_size("ctx")
    rows, columns = shard.shape
    split = shard.reshape(rows, groups, count, columns // (groups * count)).transpose(2, 0, 1, 3)
    split = after(split.reshape(count, rows, columns // count), earlier)
    mine = lax.all_to_all(split, "ctx", 0, 0, tiled=True)
    return mine.reshape(count * rows, columns // count)


def gather_rows(mine):
    return lax.all_gather(mine, FSDP, axis=0, tiled=True)


def sum_pair(left, right):
    core = lax.axis_index("core")
    grad = lax.dot_general(left, right, ROWS_FIRST, preferred_element_type=jnp.float32)
    blocks = grad.astype(jnp.bfloat16).reshape(lax.axis_size("line"), CORES, -1, grad.shape[1])
    sent = lax.dynamic_index_in_dim(blocks, CORES - 1 - core, 1, keepdims=False)
    came = lax.ppermute(sent, "core", [(0, 1), (1, 0)])
    kept = lax.dynamic_index_in_dim(blocks, core, 1, keepdims=False)
    pair = kept.astype(jnp.float32) + came.astype(jnp.float32)
    return pair.astype(jnp.bfloat16).reshape(-1, grad.shape[1])


def sum_rows(pair):
    return lax.psum_scatter(pair, "line", scatter_dimension=0, tiled=True)


def fold(value, blocks, count):
    rows, columns = value.shape
    split = value.reshape(blocks, rows // blocks, count, columns // count)
    return jnp.swapaxes(split, 1, 2).reshape(rows * count, columns // count)


def unfold(value, blocks, count):
    rows, columns = value.shape
    split = value.reshape(blocks, count, rows // (blocks * count), columns)
    return jnp.swapaxes(split, 1, 2).reshape(rows // count, columns * count)


def return_columns(summed, groups):
    count = lax.axis_size("ctx")
    rows, columns = summed.shape[0] // count, summed.shape[1]
    mine = lax.all_to_all(summed.reshape(count, rows, columns), "ctx", 0, 0, tiled=True)
    part = columns // groups
    pieces = [mine[c, :, g * part : (g + 1) * part] for g in range(groups) for c in range(count)]
    return jnp.concatenate(pieces, 1).astype(jnp.float32)


def on_device(
    tokens,
    seq_ids,
    positions,
    ln1_gain,
    ln1_bias,
    ln2_gain,
    ln2_bias,
    w_qkv,
    w_out,
    w_up,
    w_down,
    grad_out,
):
    f32 = jnp.float32
    bf16 = jnp.bfloat16
    rows = tokens.shape[1]
    ctx_count = lax.axis_size("ctx")
    fsdp_count = lax.axis_size("line") * CORES
    heads = HEADS // ctx_count
    total_rows = rows * ctx_count
    scale = HEAD_DIM ** (-0.5)

    def inner(value):
        return turn(value, ctx_count, fsdp_count)

    def outer(value):
        return turn(value, fsdp_count, ctx_count)

    out = inner(gather_rows(w_out))
    mine_qkv = exchange_columns(w_qkv, 3)
    qkv = gather_rows(mine_qkv)
    mine_up = exchange_columns(w_up, 1, mine_qkv)
    up = gather_rows(mine_up)

    gain_one = inner(ln1_gain.astype(f32))
    bias_one = inner(ln1_bias.astype(f32))
    gain_two = inner(ln2_gain.astype(f32))
    bias_two = inner(ln2_bias.astype(f32))
    own_tokens = inner(tokens[0])
    own_grads = inner(grad_out[0])
    inputs = gather_ctx(after(own_tokens, mine_up))
    layout = gather_ctx(after(jnp.stack([seq_ids[0], positions[0]], 0)[None], mine_up))
    mine_down = exchange_columns(w_down, 1, inputs)
    down = gather_rows(mine_down)
    grads = gather_ctx(after(own_grads, mine_down))
    seq = layout[:, 0].reshape(-1)
    pos = layout[:, 1].reshape(-1)

    normed, inv_std = normalize(inputs.astype(f32))
    first_in = (normed * gain_one + bias_one).astype(bf16)
    second_in = (normed * gain_two + bias_two).astype(bf16)

    projected = jnp.dot(first_in, qkv, preferred_element_type=f32)
    projected = projected.reshape(total_rows, 3, heads, HEAD_DIM)
    cosines, sines = rotary_tables(pos)
    queries = rotate(projected[:, 0], cosines, sines).astype(bf16)
    keys = rotate(projected[:, 1], cosines, sines).astype(bf16)
    values = projected[:, 2].astype(bf16)
    scores = jnp.einsum("qhd,khd->hqk", queries, keys, preferred_element_type=f32) * scale
    allowed = ((seq[:, None] == seq[None, :]) & (pos[None, :] <= pos[:, None]))[None]
    masked = jnp.where(allowed, scores, NEG_FILL)
    row_max = jnp.max(masked, axis=-1, keepdims=True)
    weights = jnp.where(allowed, jnp.exp(masked - row_max), 0.0)
    row_total = jnp.sum(weights, axis=-1, keepdims=True)
    weights = weights / row_total
    weights_low = weights.astype(bf16)
    attended = jnp.einsum("hqk,khd->qhd", weights_low, values, preferred_element_type=f32)
    attended_low = attended.reshape(total_rows, heads * HEAD_DIM).astype(bf16)
    branches = jnp.dot(attended_low, out, preferred_element_type=f32)

    grad_attended = lax.dot_general(grads, out, COLS_BOTH, preferred_element_type=f32)
    grad_attended = grad_attended.reshape(total_rows, heads, HEAD_DIM)
    delta = jnp.sum(grad_attended * attended, axis=-1).T[..., None]
    grad_heads = grad_attended.astype(bf16)
    grad_values = jnp.einsum("hqk,qhd->khd", weights_low, grad_heads, preferred_element_type=f32)
    grad_weights = jnp.einsum("qhd,khd->hqk", grad_heads, values, preferred_element_type=f32)
    grad_scores = (weights * (grad_weights - delta)).astype(bf16)
    grad_queries = (
        jnp.einsum("hqk,khd->qhd", grad_scores, keys, preferred_element_type=f32) * scale
    )
    grad_keys = jnp.einsum("hqk,qhd->khd", grad_scores, queries, preferred_element_type=f32) * scale
    grad_projected = jnp.stack(
        [
            rotate(grad_queries, cosines, -sines),
            rotate(grad_keys, cosines, -sines),
            grad_values,
        ],
        1,
    )
    grad_projected = grad_projected.reshape(total_rows, 3 * heads * HEAD_DIM).astype(bf16)
    pair_qkv = sum_pair(first_in, grad_projected)
    pair_out = sum_pair(attended_low, grads)
    lines = lax.axis_size("line")
    pair_attn = jnp.concatenate([pair_qkv, fold(pair_out, lines, ctx_count)], 1)
    summed_attn = sum_rows(pair_attn)
    summed_qkv = summed_attn[:, : qkv.shape[1]]
    summed_out = unfold(summed_attn[:, qkv.shape[1] :], 1, ctx_count)
    up = after(up, pair_attn)
    grad_first = lax.dot_general(grad_projected, qkv, COLS_BOTH, preferred_element_type=f32)

    hidden_pre = jnp.dot(second_in, up, preferred_element_type=f32)
    below = 0.5 + 0.5 * lax.erf(hidden_pre * (0.5**0.5))
    bell = jnp.exp(-0.5 * hidden_pre * hidden_pre) * (0.5 / jnp.pi) ** 0.5
    activated, slope = lax.optimization_barrier(
        ((hidden_pre * below).astype(bf16), below + hidden_pre * bell)
    )
    summed_down = sum_rows(sum_pair(grads, activated))
    grad_act = jnp.dot(grads, down, preferred_element_type=f32)
    grad_hidden = (grad_act * slope).astype(bf16)
    summed_up = sum_rows(sum_pair(second_in, grad_hidden))
    branches = branches + lax.dot_general(activated, down, COLS_BOTH, preferred_element_type=f32)
    grad_second = lax.dot_general(grad_hidden, up, COLS_BOTH, preferred_element_type=f32)

    output = scatter_ctx(branches, rows) + own_tokens.astype(f32)
    output = outer(output.astype(bf16))[None]

    norm_terms = jnp.stack(
        [
            jnp.sum(grad_first * normed, 0),
            jnp.sum(grad_first, 0),
            jnp.sum(grad_second * normed, 0),
            jnp.sum(grad_second, 0),
        ]
    )
    norm_terms = norm_terms.reshape(4, fsdp_count, ctx_count, -1).transpose(2, 1, 0, 3)
    norm_terms = norm_terms.reshape(ctx_count * fsdp_count, -1)
    norm_sums = lax.all_to_all(norm_terms, ("ctx", *FSDP), 0, 0, tiled=True)
    norm_sums = jnp.sum(norm_sums, 0).reshape(4, -1)

    scaled = scatter_ctx(grad_first * gain_one + grad_second * gain_two, rows)
    own_normed = normed[:rows]
    first_mean = jnp.mean(scaled, axis=-1, keepdims=True)
    second_mean = jnp.mean(scaled * own_normed, axis=-1, keepdims=True)
    back = (scaled - first_mean - own_normed * second_mean) * inv_std[:rows]
    grad_tokens = outer((own_grads.astype(f32) + back).astype(bf16))[None]
    return (
        output,
        grad_tokens,
        norm_sums[0],
        norm_sums[1],
        norm_sums[2],
        norm_sums[3],
        return_columns(summed_qkv, 3),
        outer(summed_out.astype(f32)),
        return_columns(summed_up, 1),
        return_columns(summed_down, 1),
    )


def solution(mesh):
    shape = (mesh.shape["ctx"], mesh.shape["fsdp"] // CORES, CORES)
    split = Mesh(np.asarray(mesh.devices).reshape(shape), ("ctx", *FSDP))
    blocks = P(FSDP, "ctx", None)
    ids = P(FSDP, "ctx")
    shards = P(("ctx", *FSDP), None)
    vector = P(("ctx", *FSDP))

    return jax.shard_map(
        on_device,
        mesh=split,
        in_specs=(blocks, ids, ids, P(), P(), P(), P(), shards, shards, shards, shards, blocks),
        out_specs=(blocks, blocks, vector, vector, vector, vector, shards, shards, shards, shards),
        check_vma=False,
    )
```

profile of v0, /device:TPU:0, one launch (start us, length us, event | category | flops | bytes accessed | tf_op | source)
XLA Modules:
  0.0 535.2 jit_solution(5037328288274787038)
XLA Ops:
  11.8 16.4 %all_to_all.40 = bf16[4,64,1536]{2,1,0:T(8,128)(2,1)} all-to-all(bf16[4,64,1536]{2,1,0:T(8,128)(2,1)S(1)} %reshape.325), channel_id=1, replica_groups=mesh['ctx'=4,'line'=4,'core'=2] {'ctx'}, dimensions={0} | all-to-all | bytes 1572864 | tf_op jit(solution)/shard_map/all_to_all | solution.py:82
  29.7 16.2 %all_to_all.41 = bf16[4,64,2048]{2,1,0:T(8,128)(2,1)} all-to-all(bf16[4,64,2048]{2,1,0:T(8,128)(2,1)S(1)} %copy.139), channel_id=1, replica_groups=mesh['ctx'=4,'line'=4,'core'=2] {'ctx'}, dimensions={0} | all-to-all | bytes 2097152 | tf_op jit(solution)/shard_map/all_to_all | solution.py:82
  59.7 14.1 %collective-permute-done.4 = s32[1,2,256]{2,1,0:T(2,128)S(1)} collective-permute-done((s32[1,2,256]{2,1,0:T(2,128)S(1)}, s32[1,2,256]{2,1,0:T(2,128)S(1)}, u32[]{:S(2)}, u32[]{:S(2)}) %collective-permute-start.4) | collective-permute-done | bytes 2080 | tf_op jit(solution)/shard_map/ppermute | solution.py:24
  78.8 4.6 collective-permute-done.2
  83.4 17.6 %collective-permute-done.1 = bf16[256,2048]{1,0:T(8,128)(2,1)S(1)} collective-permute-done((bf16[256,2048]{1,0:T(8,128)(2,1)}, bf16[256,2048]{1,0:T(8,128)(2,1)S(1)}, u32[]{:S(2)}, u32[]{:S(2)}) %collective-permute-start.1) | collective-permute-done | bytes 1048608 | tf_op jit(solution)/shard_map/ppermute | solution.py:24
  112.8 10.7 %all-to-all-done.2 = bf16[4,64,2048]{2,1,0:T(8,128)(2,1)S(1)} async-done(((bf16[4,64,2048]{2,1,0:T(8,128)(2,1)}), bf16[4,64,2048]{2,1,0:T(8,128)(2,1)S(1)}, u32[]{:S(2)}, u32[]{:S(2)}) %all-to-all-start.2) | async-done | bytes 1048608 | tf_op jit(solution)/shard_map/all_to_all | solution.py:82
  131.6 5.7 %copy.200 = bf16[512,8,4,64]{3,2,1,0:T(4,128)(2,1)} copy(bf16[512,8,4,64]{0,3,1,2:T(8,128)(2,1)S(1)} %bitcast.208) | data formatting | bytes 4194304 | tf_op jit(solution)/shard_map/dot_general | solution.py:197
  137.3 7.7 %reshape.375 = bf16[2,256,2048]{2,1,0:T(8,128)(2,1)} reshape(bf16[512,8,4,64]{3,2,1,0:T(4,128)(2,1)} %copy.200) | data formatting | bytes 4194304 | tf_op jit(solution)/shard_map/dot_general | solution.py:197
  145.0 12.3 %fusion.60 = f32[1024,1536]{1,0:T(8,128)} fusion(bf16[2048,1536]{1,0:T(8,128)(2,1)} %all-gather.5.cloned.1.call-done, bf16[1024,2048]{1,0:T(8,128)(2,1)} %get-tuple-element.68, f32[2048]{0:T(1024)S(1)} %reshape.355, f32[2048]{0:T(1024)S(1)} %reshape.354, f32[1024]{0:T(1024)S(1)} %add_rsqrt_fusion, f32[1024]{0:T(1024)S(1)} %broadcast_multiply_fusion), kind=kOutput, calls=%fused_computation.163 | convolution fusion | flops 6455033856 | bytes 16801792 | tf_op jit(solution)/shard_map/dot_general | solution.py:179
  157.4 8.2 %reshape.330 = f32[1024,3,2,256]{3,2,1,0:T(2,128)} reshape(f32[1024,1536]{1,0:T(8,128)} %fusion.60) | data formatting | bytes 12582912 | tf_op jit(solution)/shard_map/reshape | solution.py:180
  168.9 5.0 fusion.64
  184.3 10.1 %fusion.69 = (f32[2,1024]{1,0:T(2,128)S(1)}, f32[2,1024,1024]{1,2,0:T(8,128)}) fusion(pred[1024,1024]{0,1:T(8,128)(4,1)} %compare_and_fusion, bf16[1024,2,192]{2,0,1:T(8,128)(2,1)S(1)} %slice.388, bf16[1024,2,64]{2,0,1:T(8,128)(2,1)} %get-tuple-element.101, bf16[1024,2,192]{2,0,1:T(8,128)(2,1)} %slice.389, bf16[1024,2,64]{2,0,1:T(8,128)(2,1)} %get-tuple-element.100), kind=kOutput, calls=%fused_computation.171 | convolution fusion | flops 1088422912 | bytes 11542528 | tf_op jit(solution)/shard_map/sub | solution.py:189
  194.4 5.2 fusion.17
  201.9 4.6 fusion.25
  220.1 12.2 %convolution_convert_fusion.2 = bf16[2048,1536]{1,0:T(8,128)(2,1)S(1)} fusion(bf16[1024,1536]{0,1:T(8,128)(2,1)} %bitcast.242, bf16[1024,2048]{1,0:T(8,128)(2,1)} %get-tuple-element.68, f32[2048]{0:T(1024)S(1)} %reshape.355, f32[2048]{0:T(1024)S(1)} %reshape.354, f32[1024]{0:T(1024)S(1)} %add_rsqrt_fusion, f32[1024]{0:T(1024)S(1)} %broadcast_multiply_fusion), kind=kOutput, calls=%fused_computation.28 | convolution fusion | flops 6458179584 | bytes 13656064 | tf_op jit(solution)/shard_map/dot_general | solution.py:92
  235.4 5.1 convolution_convert_fusion.3
  253.1 18.3 %fusion.7 = (f32[1024,2048]{1,0:T(8,128)}, bf16[1024,2048]{1,0:T(8,128)(2,1)S(1)}) fusion(bf16[2048,2048]{1,0:T(8,128)(2,1)} %all-gather.9.cloned.1.call-done, bf16[1024,2048]{1,0:T(8,128)(2,1)} %get-tuple-element.68, f32[2048]{0:T(1024)S(1)} %reshape.357, f32[2048]{0:T(1024)S(1)} %reshape.356, f32[1024]{0:T(1024)S(1)} %add_rsqrt_fusion, ...), kind=kOutput, calls=%fused_computation.10 | convolution fusion | flops 8623489024 | bytes 25190400 | tf_op jit(solution)/shard_map/dot_general | solution.py:227
  271.4 11.9 %convolution_convert_fusion = bf16[2048,2048]{1,0:T(8,128)(2,1)S(1)} fusion(bf16[1024,2048]{1,0:T(8,128)(2,1)S(1)} %get-tuple-element.24, bf16[256,2048]{1,0:T(8,128)(2,1)} %collective-permute-done.8, bf16[256,2048]{1,0:T(8,128)(2,1)} %collective-permute-done.7, bf16[256,2048]{1,0:T(8,128)(2,1)} %collective-permute-done.6, bf16[256,2048]{1,0:T(8,128)(2,1)S(1)} %copy-done.21), kind=kOutput, calls=%fused_computation.26 | convolution fusion | flops 8610906112 | bytes 16777216 | tf_op jit(solution)/shard_map/dot_general | solution.py:92
  288.6 15.1 %multiply_convert_fusion = bf16[1024,2048]{1,0:T(8,128)(2,1)} fusion(f32[1024,2048]{1,0:T(8,128)} %get-tuple-element.25, bf16[2048,2048]{1,0:T(8,128)(2,1)} %all-gather.11.cloned.1.call-done, bf16[256,2048]{1,0:T(8,128)(2,1)} %collective-permute-done.8, bf16[256,2048]{1,0:T(8,128)(2,1)} %collective-permute-done.7, ...), kind=kOutput, calls=%fused_computation.18 | convolution fusion | flops 8610906112 | bytes 25165824 | tf_op jit(solution)/shard_map/dot_general | solution.py:234
  303.7 6.2 %fusion.8 = bf16[4,256,2048]{2,1,0:T(8,128)(2,1)} fusion(bf16[4,256,2048]{2,1,0:T(8,128)(2,1)} %collective-permute-done.18, bf16[4,2,256,2048]{3,2,1,0:T(8,128)(2,1)S(1)} %bitcast.223, s32[]{:T(128)S(6)} %select_n.24), kind=kLoop, calls=%fused_computation.12 | loop fusion | flops 8388608 | bytes 12582916 | tf_op jit(solution)/shard_map/convert_element_type | solution.py:98
  310.0 12.8 %convolution_convert_fusion.1 = bf16[2048,2048]{1,0:T(8,128)(2,1)S(1)} fusion(bf16[1024,2048]{1,0:T(8,128)(2,1)} %multiply_convert_fusion, bf16[1024,2048]{1,0:T(8,128)(2,1)} %get-tuple-element.68, f32[2048]{0:T(1024)S(1)} %reshape.357, f32[2048]{0:T(1024)S(1)} %reshape.356, f32[1024]{0:T(1024)S(1)} %add_rsqrt_fusion, f32[1024]{0:T(1024)S(1)} %broadcast_multiply_fusion), kind=kOutput, calls=%fused_computation.27 | convolution fusion | flops 8606711808 | bytes 16801792 | tf_op jit(solution)/shard_map/dot_general | solution.py:92
  325.7 12.6 %fusion.71 = f32[1024,2048]{1,0:T(8,128)S(1)} fusion(bf16[1024,2048]{1,0:T(8,128)(2,1)} %copy-done.32, bf16[2048,2048]{1,0:T(8,128)(2,1)} %all-gather.11.cloned.1.call-done), kind=kOutput, calls=%fused_computation.173 | convolution fusion | flops 8589934592 | bytes 20971520 | tf_op jit(solution)/shard_map/dot_general | solution.py:237
  338.3 5.7 %fusion.70 = (bf16[1024,2048]{1,0:T(8,128)(2,1)S(1)}, f32[1024,2048]{1,0:T(8,128)}) fusion(f32[1024,2048]{1,0:T(8,128)S(1)} %fusion.71, bf16[1024,512]{0,1:T(8,128)(2,1)S(1)} %bitcast.240, bf16[512,2048]{0,1:T(8,128)(2,1)S(1)} %bitcast.217), kind=kOutput, calls=%fused_computation.172 | convolution fusion | flops 2151677952 | bytes 24117248 | tf_op jit(solution)/shard_map/dot_general | solution.py:195
  349.2 13.5 %fusion.72 = f32[1024,2048]{1,0:T(8,128)} fusion(bf16[1024,2048]{1,0:T(8,128)(2,1)S(1)} %copy-done.31, bf16[2048,2048]{1,0:T(8,128)(2,1)} %all-gather.9.cloned.1.call-done), kind=kOutput, calls=%fused_computation.174 | convolution fusion | flops 8589934592 | bytes 20971520 | tf_op jit(solution)/shard_map/dot_general | solution.py:238
  362.8 6.4 %fusion.9 = bf16[4,256,2048]{2,1,0:T(8,128)(2,1)} fusion(bf16[4,256,2048]{2,1,0:T(8,128)(2,1)} %collective-permute-done.17, bf16[4,2,256,2048]{3,2,1,0:T(8,128)(2,1)S(1)} %bitcast.219, s32[]{:T(128)S(6)} %select_n.24), kind=kLoop, calls=%fused_computation.14 | loop fusion | flops 8388608 | bytes 12582916 | tf_op jit(solution)/shard_map/convert_element_type | solution.py:98
  371.1 18.4 %multiply_reduce_fusion.1 = (f32[2048]{0:T(1024)S(1)}, f32[2048]{0:T(1024)S(1)}, f32[2048]{0:T(1024)S(1)}, f32[2048]{0:T(1024)S(1)}, bf16[1024,2048]{1,0:T(8,128...) fusion(bf16[1024,2048]{1,0:T(8,128)(2,1)} %get-tuple-element.68, f32[1024]{0:T(1024)S(1)} %add_rsqrt_fusion, ...), kind=kOutput, calls=%fused_computation.16 | convolution fusion | flops 6469705728 | bytes 43048960 | tf_op jit(solution)/shard_map/dot_general | solution.py:225
  397.9 5.3 all-to-all-start.3
  405.3 37.9 %all-to-all-done.3 = f32[32,1,256]{2,1,0:T(1,128)S(1)} async-done(((f32[32,1,256]{2,1,0:T(1,128)}), f32[32,1,256]{2,1,0:T(1,128)S(1)}, u32[]{:S(2)}, u32[]{:S(2)}) %all-to-all-start.3) | async-done | bytes 32800 | tf_op jit(solution)/shard_map/all_to_all | solution.py:253
  455.6 4.2 all-to-all-start.4
  486.2 8.7 %all-to-all-done.6 = bf16[4,64,2048]{2,1,0:T(8,128)(2,1)S(1)} async-done(((bf16[4,64,2048]{2,1,0:T(8,128)(2,1)}), bf16[4,64,2048]{2,1,0:T(8,128)(2,1)S(1)}, u32[]{:S(2)}, u32[]{:S(2)}) %all-to-all-start.6) | async-done | bytes 1048608 | tf_op jit(solution)/shard_map/all_to_all | solution.py:120
  495.0 14.2 %reduce-scatter.6.cloned.1.call-done = bf16[256,2048]{1,0:T(8,128)(2,1)} async-done(((bf16[1024,2048]{1,0:T(8,128)(2,1)}), bf16[256,2048]{1,0:T(8,128)(2,1)}) %reduce-scatter.6.cloned.1.call-update) | async-done | bytes 1048592 | tf_op jit(solution)/shard_map/reduce_scatter | solution.py:102
  514.3 12.0 %all-to-all-done.5 = bf16[4,64,2048]{2,1,0:T(8,128)(2,1)S(1)} async-done(((bf16[4,64,2048]{2,1,0:T(8,128)(2,1)}), bf16[4,64,2048]{2,1,0:T(8,128)(2,1)S(1)}, u32[]{:S(2)}, u32[]{:S(2)}) %all-to-all-start.5) | async-done | bytes 1048608 | tf_op jit(solution)/shard_map/all_to_all | solution.py:120
  (253 shorter events, 160.9 us)
Async XLA Ops:
  7.2 121.5 %all-gather.7.cloned.1.call-start = ((), (), s32[]{:S(2)}) async-start(), calls=%async_computation.11 | async-start | bytes 2359296 | tf_op jit(solution)/shard_map/all_gather | solution.py:87
  7.9 137.1 %all-gather.5.cloned.1.call-start = ((), (), s32[]{:S(2)}) async-start(), calls=%async_computation.10 | async-start | bytes 7077888 | tf_op jit(solution)/shard_map/all_gather | solution.py:87
  28.3 224.8 %all-gather.9.cloned.1.call-start = ((), (), s32[]{:S(2)}) async-start(), calls=%async_computation.12 | async-start | bytes 9437184 | tf_op jit(solution)/shard_map/all_gather | solution.py:87
  51.2 7.3 %collective-permute-start.3 = (s32[1,2,256]{2,1,0:T(2,128)S(1)}, s32[1,2,256]{2,1,0:T(2,128)S(1)}, u32[]{:S(2)}, u32[]{:S(2)}) collective-permute-start(s32[1,2,256]{2,1,0:T(2,128)S(1)} %add_bitcast_fusion), channel_id=1, source_target_pairs={{0,8},{8,0},{16,24},{24,16},{1,9},{9,1},{17,25},{25,17},{2,10},{10... | collective-permute-start | bytes 6152 | tf_op jit(solution)/shard_map/ppermute | solution.py:24
  52.2 21.6 %collective-permute-start.5 = (s32[1,2,256]{2,1,0:T(2,128)S(1)}, s32[1,2,256]{2,1,0:T(2,128)S(1)}, u32[]{:S(2)}, u32[]{:S(2)}) collective-permute-start(s32[1,2,256]{2,1,0:T(2,128)S(1)} %add_bitcast_fusion), channel_id=1, source_target_pairs={{0,24},{8,16},{16,8},{24,0},{1,25},{9,17},{17,9},{25,1},{2,26},{10... | collective-permute-start | bytes 6152 | tf_op jit(solution)/shard_map/ppermute | solution.py:24
  53.7 20.1 %collective-permute-start.4 = (s32[1,2,256]{2,1,0:T(2,128)S(1)}, s32[1,2,256]{2,1,0:T(2,128)S(1)}, u32[]{:S(2)}, u32[]{:S(2)}) collective-permute-start(s32[1,2,256]{2,1,0:T(2,128)S(1)} %add_bitcast_fusion), channel_id=1, source_target_pairs={{0,16},{8,24},{16,0},{24,8},{1,17},{9,25},{17,1},{25,9},{2,18},{10... | collective-permute-start | bytes 6152 | tf_op jit(solution)/shard_map/ppermute | solution.py:24
  56.2 27.1 %collective-permute-start.2 = (bf16[256,2048]{1,0:T(8,128)(2,1)}, bf16[256,2048]{1,0:T(8,128)(2,1)S(1)}, u32[]{:S(2)}, u32[]{:S(2)}) collective-permute-start(bf16[256,2048]{1,0:T(8,128)(2,1)} %copy.143), channel_id=1, source_target_pairs={{0,24},{8,16},{16,8},{24,0},{1,25},{9,17},{17,9},{25,1},{2,26},{10... | collective-permute-start | bytes 3145736 | tf_op jit(solution)/shard_map/ppermute | solution.py:24
  57.1 43.9 %collective-permute-start.1 = (bf16[256,2048]{1,0:T(8,128)(2,1)}, bf16[256,2048]{1,0:T(8,128)(2,1)S(1)}, u32[]{:S(2)}, u32[]{:S(2)}) collective-permute-start(bf16[256,2048]{1,0:T(8,128)(2,1)} %copy.143), channel_id=1, source_target_pairs={{0,16},{8,24},{16,0},{24,8},{1,17},{9,25},{17,1},{25,9},{2,18},{10... | collective-permute-start | bytes 3145736 | tf_op jit(solution)/shard_map/ppermute | solution.py:24
  58.6 42.4 %collective-permute-start = (bf16[256,2048]{1,0:T(8,128)(2,1)}, bf16[256,2048]{1,0:T(8,128)(2,1)S(1)}, u32[]{:S(2)}, u32[]{:S(2)}) collective-permute-start(bf16[256,2048]{1,0:T(8,128)(2,1)} %copy.143), channel_id=1, source_target_pairs={{0,8},{8,0},{16,24},{24,16},{1,9},{9,1},{17,25},{25,17},{2,10},{10... | collective-permute-start | bytes 3145736 | tf_op jit(solution)/shard_map/ppermute | solution.py:24
  105.8 17.7 %all-to-all-start.2 = ((bf16[4,64,2048]{2,1,0:T(8,128)(2,1)}), bf16[4,64,2048]{2,1,0:T(8,128)(2,1)S(1)}, u32[]{:S(2)}, u32[]{:S(2)}) async-start(bf16[4,64,2048]{2,1,0:T(8,128)(2,1)} %copy.156), calls=%async_computation.2 | async-start | bytes 2097152 | tf_op jit(solution)/shard_map/all_to_all | solution.py:82
  109.3 179.3 %all-gather.11.cloned.1.call-start = ((), (), s32[]{:S(2)}) async-start(), calls=%async_computation.13 | async-start | bytes 9437184 | tf_op jit(solution)/shard_map/all_gather | solution.py:87
  112.8 292.5 %copy-start.24 = (f32[1024]{0:T(1024)}, f32[1024]{0:T(1024)S(1)}, u32[]{:S(2)}) copy-start(f32[1024]{0:T(1024)S(1)} %add_rsqrt_fusion) | copy-start | bytes 12292
  124.9 76.9 %collective-permute-start.8 = (bf16[256,2048]{1,0:T(8,128)(2,1)}, bf16[256,2048]{1,0:T(8,128)(2,1)}, u32[]{:S(2)}, u32[]{:S(2)}) collective-permute-start(bf16[256,2048]{1,0:T(8,128)(2,1)} %copy.160), channel_id=1, source_target_pairs={{0,24},{8,16},{16,8},{24,0},{1,25},{9,17},{17,9},{25,1},{2,26},{10... | collective-permute-start | bytes 3145736 | tf_op jit(solution)/shard_map/ppermute | solution.py:24
  126.3 75.5 %collective-permute-start.7 = (bf16[256,2048]{1,0:T(8,128)(2,1)}, bf16[256,2048]{1,0:T(8,128)(2,1)}, u32[]{:S(2)}, u32[]{:S(2)}) collective-permute-start(bf16[256,2048]{1,0:T(8,128)(2,1)} %copy.160), channel_id=1, source_target_pairs={{0,16},{8,24},{16,0},{24,8},{1,17},{9,25},{17,1},{25,9},{2,18},{10... | collective-permute-start | bytes 3145736 | tf_op jit(solution)/shard_map/ppermute | solution.py:24
  127.8 74.1 %collective-permute-start.6 = (bf16[256,2048]{1,0:T(8,128)(2,1)}, bf16[256,2048]{1,0:T(8,128)(2,1)}, u32[]{:S(2)}, u32[]{:S(2)}) collective-permute-start(bf16[256,2048]{1,0:T(8,128)(2,1)} %copy.160), channel_id=1, source_target_pairs={{0,8},{8,0},{16,24},{24,16},{1,9},{9,1},{17,25},{25,17},{2,10},{10... | collective-permute-start | bytes 3145736 | tf_op jit(solution)/shard_map/ppermute | solution.py:24
  128.4 325.1 %reduce-scatter.4.cloned.1.call-start = ((), (), s32[]{:S(2)}) async-start(), calls=%async_computation.14 | async-start | bytes 5242880 | tf_op jit(solution)/shard_map/reduce_scatter | solution.py:102
  234.3 12.3 %collective-permute-start.9 = (bf16[4,256,1536]{2,1,0:T(8,128)(2,1)}, bf16[4,256,1536]{2,1,0:T(8,128)(2,1)}, u32[]{:S(2)}, u32[]{:S(2)}) collective-permute-start(bf16[4,256,1536]{2,1,0:T(8,128)(2,1)} %dynamic-slice_bitcast_fusion.2), channel_id=1, source_target_pairs={{0,1},{1,0},{2,3},{3,2},{4,5},{5,4},{6,7},{7,6},{8,9},{9,8},{10,11... | collective-permute-start | bytes 9437192 | tf_op jit(solution)/shard_map/ppermute | solution.py:95
  241.5 3.4 collective-permute-start.10
  253.0 225.1 %reduce-scatter.8.cloned.1.call-start = ((), (), s32[]{:S(2)}) async-start(), calls=%async_computation.16 | async-start | bytes 5242880 | tf_op jit(solution)/shard_map/reduce_scatter | solution.py:102
  288.2 15.5 %collective-permute-start.18 = (bf16[4,256,2048]{2,1,0:T(8,128)(2,1)}, bf16[4,256,2048]{2,1,0:T(8,128)(2,1)}, u32[]{:S(2)}, u32[]{:S(2)}) collective-permute-start(bf16[4,256,2048]{2,1,0:T(8,128)(2,1)} %dynamic-slice_bitcast_fusion), channel_id=1, source_target_pairs={{0,1},{1,0},{2,3},{3,2},{4,5},{5,4},{6,7},{7,6},{8,9},{9,8},{10,11... | collective-permute-start | bytes 12582920 | tf_op jit(solution)/shard_map/ppermute | solution.py:95
  309.9 199.3 %reduce-scatter.6.cloned.1.call-start = ((), (), s32[]{:S(2)}) async-start(), calls=%async_computation.15 | async-start | bytes 5242880 | tf_op jit(solution)/shard_map/reduce_scatter | solution.py:102
  325.3 37.5 %collective-permute-start.17 = (bf16[4,256,2048]{2,1,0:T(8,128)(2,1)}, bf16[4,256,2048]{2,1,0:T(8,128)(2,1)}, u32[]{:S(2)}, u32[]{:S(2)}) collective-permute-start(bf16[4,256,2048]{2,1,0:T(8,128)(2,1)} %dynamic-slice_bitcast_fusion.1), channel_id=1, source_target_pairs={{0,1},{1,0},{2,3},{3,2},{4,5},{5,4},{6,7},{7,6},{8,9},{9,8},{10,11... | collective-permute-start | bytes 12582920 | tf_op jit(solution)/shard_map/ppermute | solution.py:95
  345.7 50.6 %collective-permute-start.11 = (bf16[256,2048]{1,0:T(8,128)(2,1)}, bf16[256,2048]{1,0:T(8,128)(2,1)}, u32[]{:S(2)}, u32[]{:S(2)}) collective-permute-start(bf16[256,2048]{1,0:T(8,128)(2,1)} %get-tuple-element.79), channel_id=1, source_target_pairs={{0,8},{8,0},{16,24},{24,16},{1,9},{9,1},{17,25},{25,17},{2,10},{10... | collective-permute-start | bytes 3145736 | tf_op jit(solution)/shard_map/ppermute | solution.py:24
  347.3 96.6 %collective-permute-start.13 = (bf16[256,2048]{1,0:T(8,128)(2,1)}, bf16[256,2048]{1,0:T(8,128)(2,1)}, u32[]{:S(2)}, u32[]{:S(2)}) collective-permute-start(bf16[256,2048]{1,0:T(8,128)(2,1)} %get-tuple-element.80), channel_id=1, source_target_pairs={{0,24},{8,16},{16,8},{24,0},{1,25},{9,17},{17,9},{25,1},{2,26},{10... | collective-permute-start | bytes 3145736 | tf_op jit(solution)/shard_map/ppermute | solution.py:24
  348.8 95.1 %collective-permute-start.12 = (bf16[256,2048]{1,0:T(8,128)(2,1)}, bf16[256,2048]{1,0:T(8,128)(2,1)}, u32[]{:S(2)}, u32[]{:S(2)}) collective-permute-start(bf16[256,2048]{1,0:T(8,128)(2,1)} %get-tuple-element.81), channel_id=1, source_target_pairs={{0,16},{8,24},{16,0},{24,8},{1,17},{9,25},{17,1},{25,9},{2,18},{10... | collective-permute-start | bytes 3145736 | tf_op jit(solution)/shard_map/ppermute | solution.py:24
  393.3 56.3 %collective-permute-start.14 = (bf16[256,2048]{1,0:T(8,128)(2,1)}, bf16[256,2048]{1,0:T(8,128)(2,1)}, u32[]{:S(2)}, u32[]{:S(2)}) collective-permute-start(bf16[256,2048]{1,0:T(8,128)(2,1)} %get-tuple-element.76), channel_id=1, source_target_pairs={{0,8},{8,0},{16,24},{24,16},{1,9},{9,1},{17,25},{25,17},{2,10},{10... | collective-permute-start | bytes 3145736 | tf_op jit(solution)/shard_map/ppermute | solution.py:24
  394.9 54.7 %collective-permute-start.16 = (bf16[256,2048]{1,0:T(8,128)(2,1)}, bf16[256,2048]{1,0:T(8,128)(2,1)}, u32[]{:S(2)}, u32[]{:S(2)}) collective-permute-start(bf16[256,2048]{1,0:T(8,128)(2,1)} %get-tuple-element.77), channel_id=1, source_target_pairs={{0,24},{8,16},{16,8},{24,0},{1,25},{9,17},{17,9},{25,1},{2,26},{10... | collective-permute-start | bytes 3145736 | tf_op jit(solution)/shard_map/ppermute | solution.py:24
  396.3 53.2 %collective-permute-start.15 = (bf16[256,2048]{1,0:T(8,128)(2,1)}, bf16[256,2048]{1,0:T(8,128)(2,1)}, u32[]{:S(2)}, u32[]{:S(2)}) collective-permute-start(bf16[256,2048]{1,0:T(8,128)(2,1)} %get-tuple-element.78), channel_id=1, source_target_pairs={{0,16},{8,24},{16,0},{24,8},{1,17},{9,25},{17,1},{25,9},{2,18},{10... | collective-permute-start | bytes 3145736 | tf_op jit(solution)/shard_map/ppermute | solution.py:24
  397.9 45.3 %all-to-all-start.3 = ((f32[32,1,256]{2,1,0:T(1,128)}), f32[32,1,256]{2,1,0:T(1,128)S(1)}, u32[]{:S(2)}, u32[]{:S(2)}) async-start(f32[32,1,256]{2,1,0:T(1,128)} %all_to_all.32), calls=%async_computation.3 | async-start | bytes 65536 | tf_op jit(solution)/shard_map/all_to_all | solution.py:253
  455.6 15.7 %all-to-all-start.4 = ((bf16[4,64,1536]{2,1,0:T(8,128)(2,1)}), bf16[4,64,1536]{2,1,0:T(8,128)(2,1)}, u32[]{:S(2)}, u32[]{:S(2)}) async-start(bf16[4,64,1536]{2,1,0:T(8,128)(2,1)} %bitcast.245), calls=%async_computation.5 | async-start | bytes 1572864 | tf_op jit(solution)/shard_map/all_to_all | solution.py:120
  478.1 16.9 %all-to-all-start.6 = ((bf16[4,64,2048]{2,1,0:T(8,128)(2,1)}), bf16[4,64,2048]{2,1,0:T(8,128)(2,1)S(1)}, u32[]{:S(2)}, u32[]{:S(2)}) async-start(bf16[4,64,2048]{2,1,0:T(8,128)(2,1)} %bitcast.249), calls=%async_computation.9 | async-start | bytes 2097152 | tf_op jit(solution)/shard_map/all_to_all | solution.py:120
  509.2 17.1 %all-to-all-start.5 = ((bf16[4,64,2048]{2,1,0:T(8,128)(2,1)}), bf16[4,64,2048]{2,1,0:T(8,128)(2,1)S(1)}, u32[]{:S(2)}, u32[]{:S(2)}) async-start(bf16[4,64,2048]{2,1,0:T(8,128)(2,1)} %bitcast.250), calls=%async_computation.7 | async-start | bytes 2097152 | tf_op jit(solution)/shard_map/all_to_all | solution.py:120
  (36 other events, 365.9 us)
Sparse Core Ops, SparseCore 0:
  9.6 31.8 all-gather.6
  43.1 64.0 all-gather.4
  108.9 80.6 all-gather.8
  191.6 80.5 all-gather.10
  274.3 75.2 reduce-scatter.3
  351.8 77.7 reduce-scatter.7
  431.9 77.2 reduce-scatter.5
where the time goes:
time: 545 us; the launch traced here: 535 us
  matrix products  161 us (30%)
  waiting for transfers between devices  127 us (23%)
  local copies, waits for them, and re-layouts  103 us (19%)
  other arithmetic  57.6 us (11%)
  starting transfers between devices  38.8 us (7%)
  blocking collectives  32.6 us (6%)
  between operations  15.5 us (3%)
    dot_general x4, matrix products, sum_pair(): lax.dot_general(left, right, ROWS_FIRST, preferred_element_type=jnp.float32)  42 us
    all_to_all x1, waiting for transfers between devices, on_device(): norm_sums = lax.all_to_all(norm_terms, ('ctx', *FSDP), 0, 0, tiled=True)  37.9 us
    ppermute x15, waiting for transfers between devices, swap(): return lax.ppermute(value, 'ctx', [(i, i ^ step) for i in range(count)])  36.3 us
    all_to_all x2, blocking collectives, exchange_columns(): mine = lax.all_to_all(split, 'ctx', 0, 0, tiled=True)  32.6 us
    unnamed x89, local copies, waits for them, and re-layouts  25.2 us
    all_to_all x3, waiting for transfers between devices, return_columns(): lax.all_to_all(summed.reshape(count, rows, columns), 'ctx', 0, 0, tiled=T...  23.6 us
    dot_general x1, matrix products, on_device(): lax.dot_general(grad_projected, qkv, COLS_BOTH, preferred_element_type=f32)  18.4 us
    dot_general x1, matrix products, on_device(): hidden_pre = jnp.dot(second_in, up, preferred_element_type=f32)  18.3 us
  transfers between devices with their start and end apart: 31, of which 10 were waited for; matrix products, arithmetic and copies ran while one was open for 59% of the time, Pallas kernels for 0%

commit v1 on v0

--- a/solution.py
+++ b/solution.py
@@ -24,17 +24,18 @@
     return lax.ppermute(value, "ctx", [(i, i ^ step) for i in range(count)])
 
 
-def gather_ctx(block):
-    count = lax.axis_size("ctx")
-    return jnp.concatenate([block] + [swap(block, k) for k in range(1, count)], 0)
-
-
-def scatter_ctx(parts, rows):
-    count = lax.axis_size("ctx")
-    low = parts.astype(jnp.bfloat16)
-    total = parts[:rows]
-    for k in range(1, count):
-        total = total + swap(low[k * rows : (k + 1) * rows], k).astype(jnp.float32)
+def blocks_of_ctx(block):
+    count = lax.axis_size("ctx")
+    return (block, *(swap(block, k) for k in range(1, count)))
+
+
+def scatter_ctx(low, rows, until):
+    count = lax.axis_size("ctx")
+    came = [swap(low[k * rows : (k + 1) * rows], k) for k in range(1, count)]
+    came = after(tuple(came), until)
+    total = low[:rows].astype(jnp.float32)
+    for part in came:
+        total = total + part.astype(jnp.float32)
     return total
 
 
@@ -155,8 +156,8 @@
     out = inner(gather_rows(w_out))
     mine_qkv = exchange_columns(w_qkv, 3)
     qkv = gather_rows(mine_qkv)
-    mine_up = exchange_columns(w_up, 1, mine_qkv)
-    up = gather_rows(mine_up)
+    mine_mlp = exchange_columns(jnp.concatenate([w_up, w_down], 1), 2, mine_qkv)
+    mlp = gather_rows(mine_mlp)
 
     gain_one = inner(ln1_gain.astype(f32))
     bias_one = inner(ln1_bias.astype(f32))
@@ -164,19 +165,20 @@
     bias_two = inner(ln2_bias.astype(f32))
     own_tokens = inner(tokens[0])
     own_grads = inner(grad_out[0])
-    inputs = gather_ctx(after(own_tokens, mine_up))
-    layout = gather_ctx(after(jnp.stack([seq_ids[0], positions[0]], 0)[None], mine_up))
-    mine_down = exchange_columns(w_down, 1, inputs)
-    down = gather_rows(mine_down)
-    grads = gather_ctx(after(own_grads, mine_down))
+    inputs = jnp.concatenate(blocks_of_ctx(after(own_tokens, mine_mlp)), 0)
+    layout = after(jnp.stack([seq_ids[0], positions[0]], 0)[None], mine_mlp)
+    layout = jnp.concatenate(blocks_of_ctx(layout), 0)
+    grad_blocks = blocks_of_ctx(after(own_grads, inputs))
     seq = layout[:, 0].reshape(-1)
     pos = layout[:, 1].reshape(-1)
 
+    inputs, out = lax.optimization_barrier((inputs, out))
     normed, inv_std = normalize(inputs.astype(f32))
     first_in = (normed * gain_one + bias_one).astype(bf16)
     second_in = (normed * gain_two + bias_two).astype(bf16)
 
     projected = jnp.dot(first_in, qkv, preferred_element_type=f32)
+    grads = jnp.concatenate(after(grad_blocks, projected), 0)
     projected = projected.reshape(total_rows, 3, heads, HEAD_DIM)
     cosines, sines = rotary_tables(pos)
     queries = rotate(projected[:, 0], cosines, sines).astype(bf16)
@@ -192,7 +194,6 @@
     weights_low = weights.astype(bf16)
     attended = jnp.einsum("hqk,khd->qhd", weights_low, values, preferred_element_type=f32)
     attended_low = attended.reshape(total_rows, heads * HEAD_DIM).astype(bf16)
-    branches = jnp.dot(attended_low, out, preferred_element_type=f32)
 
     grad_attended = lax.dot_general(grads, out, COLS_BOTH, preferred_element_type=f32)
     grad_attended = grad_attended.reshape(total_rows, heads, HEAD_DIM)
@@ -219,27 +220,39 @@
     lines = lax.axis_size("line")
     pair_attn = jnp.concatenate([pair_qkv, fold(pair_out, lines, ctx_count)], 1)
     summed_attn = sum_rows(pair_attn)
-    summed_qkv = summed_attn[:, : qkv.shape[1]]
-    summed_out = unfold(summed_attn[:, qkv.shape[1] :], 1, ctx_count)
-    up = after(up, pair_attn)
-    grad_first = lax.dot_general(grad_projected, qkv, COLS_BOTH, preferred_element_type=f32)
+    mlp = after(mlp, pair_attn)
+    half = mlp.shape[1] // 2
+    up = mlp[:, :half]
 
     hidden_pre = jnp.dot(second_in, up, preferred_element_type=f32)
     below = 0.5 + 0.5 * lax.erf(hidden_pre * (0.5**0.5))
     bell = jnp.exp(-0.5 * hidden_pre * hidden_pre) * (0.5 / jnp.pi) ** 0.5
-    activated, slope = lax.optimization_barrier(
-        ((hidden_pre * below).astype(bf16), below + hidden_pre * bell)
-    )
-    summed_down = sum_rows(sum_pair(grads, activated))
-    grad_act = jnp.dot(grads, down, preferred_element_type=f32)
+    active = (hidden_pre * below).astype(bf16)
+    slope = below + hidden_pre * bell
+    activated, slope = lax.optimization_barrier((active, slope))
+    pair_down = sum_pair(grads, activated)
+    summed_down = sum_rows(pair_down)
+    mlp = after(mlp, pair_down)
+    grad_act = jnp.dot(grads, mlp[:, half:], preferred_element_type=f32)
     grad_hidden = (grad_act * slope).astype(bf16)
-    summed_up = sum_rows(sum_pair(second_in, grad_hidden))
-    branches = branches + lax.dot_general(activated, down, COLS_BOTH, preferred_element_type=f32)
-    grad_second = lax.dot_general(grad_hidden, up, COLS_BOTH, preferred_element_type=f32)
-
-    output = scatter_ctx(branches, rows) + own_tokens.astype(f32)
+    branches = jnp.dot(attended_low, out, preferred_element_type=f32)
+    down_part = lax.dot_general(
+        activated, mlp[:, half:], COLS_BOTH, preferred_element_type=f32
+    )
+    branches = (branches + down_part).astype(bf16)
+    grad_hidden = after(grad_hidden, branches)
+    pair_up = sum_pair(second_in, grad_hidden)
+    summed_up = sum_rows(pair_up)
+    output = scatter_ctx(branches, rows, pair_up) + own_tokens.astype(f32)
     output = outer(output.astype(bf16))[None]
 
+    mlp, qkv, summed_attn = lax.optimization_barrier((mlp, qkv, summed_attn, pair_up))[:3]
+    summed_qkv = summed_attn[:, : qkv.shape[1]]
+    summed_out = unfold(summed_attn[:, qkv.shape[1] :], 1, ctx_count)
+    grad_second = lax.dot_general(grad_hidden, mlp[:, :half], COLS_BOTH, preferred_element_type=f32)
+    grad_first = lax.dot_general(grad_projected, qkv, COLS_BOTH, preferred_element_type=f32)
+    scaled = (grad_first * gain_one + grad_second * gain_two).astype(bf16)
+    grad_first, grad_second, scaled = lax.optimization_barrier((grad_first, grad_second, scaled))
     norm_terms = jnp.stack(
         [
             jnp.sum(grad_first * normed, 0),
@@ -248,12 +261,12 @@
             jnp.sum(grad_second, 0),
         ]
     )
+    scaled = scatter_ctx(scaled, rows, norm_terms)
     norm_terms = norm_terms.reshape(4, fsdp_count, ctx_count, -1).transpose(2, 1, 0, 3)
     norm_terms = norm_terms.reshape(ctx_count * fsdp_count, -1)
     norm_sums = lax.all_to_all(norm_terms, ("ctx", *FSDP), 0, 0, tiled=True)
     norm_sums = jnp.sum(norm_sums, 0).reshape(4, -1)
 
-    scaled = scatter_ctx(grad_first * gain_one + grad_second * gain_two, rows)
     own_normed = normed[:rows]
     first_mean = jnp.mean(scaled, axis=-1, keepdims=True)
     second_mean = jnp.mean(scaled * own_normed, axis=-1, keepdims=True)

time: 545 us -> 563 us (1.033)
  other arithmetic: 57.6 us -> 70 us
  blocking collectives: 32.6 us -> 43.9 us
  matrix products: 161 us -> 153 us
    ppermute x15, waiting for transfers between devices: 36.3 us -> 94.6 us  [swap(): return lax.ppermute(value, 'ctx', [(i, i ^ step) for i in range(count)])]
    all_to_all x1, waiting for transfers between devices: 37.9 us -> 0.01 us  [on_device(): norm_sums = lax.all_to_all(norm_terms, ('ctx', *FSDP), 0, 0, tiled=True)]
    dot_general x2 -> x0, local copies, waits for them, and re-layouts: 13.4 us -> none  [on_device(): lax.dot_general(grads, out, COLS_BOTH, preferred_element_type=f32)]
    unnamed x89 -> x110, local copies, waits for them, and re-layouts: 25.2 us -> 37.9 us
    reduce_scatter x3, waiting for transfers between devices: 14.2 us -> 1.87 us  [sum_rows(): return lax.psum_scatter(pair, 'line', scatter_dimension=0, tiled=True)]
    all_to_all x2, blocking collectives: 32.6 us -> 43.9 us  [exchange_columns(): mine = lax.all_to_all(split, 'ctx', 0, 0, tiled=True)]
    all_to_all x1 -> x0, waiting for transfers between devices: 10.7 us -> none  [exchange_columns(): mine = lax.all_to_all(split, 'ctx', 0, 0, tiled=True)]
    reduce_sum x0 -> x1, other arithmetic: none -> 9.32 us  [on_device(): jnp.sum(grad_first * normed, 0)]
  transfers between devices with their start and end apart: 31 -> 29, of which waited for: 10 -> 14; matrix products, arithmetic and copies ran while one was open for 59% -> 50% of each run, Pallas kernels for 0% -> 0%
where the time goes in v1:
time: 563 us; the launch traced here: 557 us
  matrix products  153 us (27%)
  waiting for transfers between devices  132 us (23%)
  local copies, waits for them, and re-layouts  106 us (19%)
  other arithmetic  70 us (12%)
  blocking collectives  43.9 us (8%)
  starting transfers between devices  36.1 us (6%)
  between operations  15.2 us (3%)
    ppermute x15, waiting for transfers between devices, swap(): return lax.ppermute(value, 'ctx', [(i, i ^ step) for i in range(count)])  94.6 us
    all_to_all x2, blocking collectives, exchange_columns(): mine = lax.all_to_all(split, 'ctx', 0, 0, tiled=True)  43.9 us
    unnamed x110, local copies, waits for them, and re-layouts  37.9 us
    dot_general x4, matrix products, sum_pair(): lax.dot_general(left, right, ROWS_FIRST, preferred_element_type=jnp.float32)  34.2 us
    all_to_all x3, waiting for transfers between devices, return_columns(): lax.all_to_all(summed.reshape(count, rows, columns), 'ctx', 0, 0, tiled=T...  25.3 us
    convert_element_type x4, other arithmetic, sum_pair(): return pair.astype(jnp.bfloat16).reshape(-1, grad.shape[1])  21.4 us
    dot_general x1, matrix products, on_device(): hidden_pre = jnp.dot(second_in, up, preferred_element_type=f32)  19.2 us
    ppermute x15, starting transfers between devices, swap(): return lax.ppermute(value, 'ctx', [(i, i ^ step) for i in range(count)])  17.6 us
  transfers between devices with their start and end apart: 29, of which 14 were waited for; matrix products, arithmetic and copies ran while one was open for 50% of the time, Pallas kernels for 0%

profile of v1, /device:TPU:0, one launch (start us, length us, event | category | flops | bytes accessed | tf_op | source)
XLA Modules:
  0.0 556.5 jit_solution(10333518124802182001)
XLA Ops:
  11.8 16.4 %all_to_all.35 = bf16[4,64,1536]{2,1,0:T(8,128)(2,1)} all-to-all(bf16[4,64,1536]{2,1,0:T(8,128)(2,1)S(1)} %reshape.315), channel_id=1, replica_groups=mesh['ctx'=4,'line'=4,'core'=2] {'ctx'}, dimensions={0} | all-to-all | bytes 1572864 | tf_op jit(solution)/shard_map/all_to_all | solution.py:83
  41.2 27.5 %all_to_all.36 = bf16[4,64,4096]{2,1,0:T(8,128)(2,1)} all-to-all(bf16[4,64,4096]{2,1,0:T(8,128)(2,1)S(1)} %reshape.313), channel_id=1, replica_groups=mesh['ctx'=4,'line'=4,'core'=2] {'ctx'}, dimensions={0} | all-to-all | bytes 4194304 | tf_op jit(solution)/shard_map/all_to_all | solution.py:83
  80.0 14.3 %collective-permute-done.4 = s32[1,2,256]{2,1,0:T(2,128)S(1)} collective-permute-done((s32[1,2,256]{2,1,0:T(2,128)S(1)}, s32[1,2,256]{2,1,0:T(2,128)S(1)}, u32[]{:S(2)}, u32[]{:S(2)}) %collective-permute-start.4) | collective-permute-done | bytes 2080 | tf_op jit(solution)/shard_map/ppermute | solution.py:24
  99.6 3.8 collective-permute-done.2
  103.4 17.8 %collective-permute-done.1 = bf16[256,2048]{1,0:T(8,128)(2,1)S(1)} collective-permute-done((bf16[256,2048]{1,0:T(8,128)(2,1)S(1)}, bf16[256,2048]{1,0:T(8,128)(2,1)S(1)}, u32[]{:S(2)}, u32[]{:S(2)}) %collective-permute-start.1) | collective-permute-done | bytes 1048608 | tf_op jit(solution)/shard_map/ppermute | solution.py:24
  134.7 12.4 %fusion.62 = f32[1024,1536]{1,0:T(8,128)} fusion(bf16[2048,1536]{1,0:T(8,128)(2,1)} %all-gather.6.cloned.1.call-done, bf16[1024,2048]{1,0:T(8,128)(2,1)} %pad_maximum_fusion, f32[2048]{0:T(1024)S(1)} %reshape.343, f32[2048]{0:T(1024)S(1)} %reshape.342, f32[1024]{0:T(1024)S(1)} %add_rsqrt_fusion, f32[1024]{0:T(1024)S(1)} %broadcast_multiply_fusion), kind=kOutput, calls=%fused_computation.168 | convolution fusion | flops 6455033856 | bytes 16801792 | tf_op jit(solution)/shard_map/dot_general | solution.py:180
  147.1 8.2 %reshape.322 = f32[1024,3,2,256]{3,2,1,0:T(2,128)} reshape(f32[1024,1536]{1,0:T(8,128)} %fusion.62) | data formatting | bytes 12582912 | tf_op jit(solution)/shard_map/reshape | solution.py:182
  155.3 16.8 %collective-permute-done.7 = bf16[256,2048]{0,1:T(8,128)(2,1)} collective-permute-done((bf16[256,2048]{0,1:T(8,128)(2,1)S(1)}, bf16[256,2048]{0,1:T(8,128)(2,1)}, u32[]{:S(2)}, u32[]{:S(2)}) %collective-permute-start.7) | collective-permute-done | bytes 1048608 | tf_op jit(solution)/shard_map/ppermute | solution.py:24
  194.3 10.3 %fusion.68 = (f32[2,1024]{1,0:T(2,128)S(1)}, f32[2,1024,1024]{1,2,0:T(8,128)}) fusion(pred[1024,1024]{0,1:T(8,128)(4,1)} %compare_and_fusion, bf16[1024,2,192]{2,0,1:T(8,128)(2,1)} %slice.399, bf16[1024,2,64]{2,0,1:T(8,128)(2,1)S(1)} %get-tuple-element.132, bf16[1024,2,192]{2,0,1:T(8,128)(2,1)} %slice.400, bf16[1024,2,64]{2,0,1:T(8,128)(2,1)} %get-tuple-element.131), kind=kOutput, calls=%fused_computation.174 | convolution fusion | flops 1088422912 | bytes 11542528 | tf_op jit(solution)/shard_map/sub | solution.py:191
  204.6 5.3 fusion.25
  227.6 12.1 %convolution_convert_fusion.2 = bf16[2048,1536]{1,0:T(8,128)(2,1)S(1)} fusion(bf16[1024,1536]{0,1:T(8,128)(2,1)} %bitcast.231, bf16[1024,2048]{1,0:T(8,128)(2,1)} %pad_maximum_fusion, f32[2048]{0:T(1024)S(1)} %reshape.343, f32[2048]{0:T(1024)S(1)} %reshape.342, f32[1024]{0:T(1024)S(1)} %add_rsqrt_fusion, f32[1024]{0:T(1024)S(1)} %broadcast_multiply_fusion), kind=kOutput, calls=%fused_computation.33 | convolution fusion | flops 6458179584 | bytes 13656064 | tf_op jit(solution)/shard_map/dot_general | solution.py:93
  260.6 19.2 %fusion.7 = (f32[1024,2048]{1,0:T(8,128)}, bf16[1024,2048]{1,0:T(8,128)(2,1)S(1)}) fusion(bf16[2048,4096]{1,0:T(8,128)(2,1)} %all-gather.8.cloned.1.call-done, bf16[1024,2048]{1,0:T(8,128)(2,1)} %pad_maximum_fusion, f32[2048]{0:T(1024)S(1)} %reshape.345, f32[2048]{0:T(1024)S(1)} %reshape.344, f32[1024]{0:T(1024)S(1)} %add_rsqrt_fusion, ...), kind=kOutput, calls=%fused_computation.10 | convolution fusion | flops 8623489024 | bytes 25190400 | tf_op jit(solution)/shard_map/dot_general | solution.py:227
  279.8 9.4 %convolution_convert_fusion.1 = bf16[2048,2048]{1,0:T(8,128)(2,1)S(1)} fusion(bf16[1024,2048]{0,1:T(8,128)(2,1)S(1)} %copy-done.33, bf16[1024,2048]{1,0:T(8,128)(2,1)S(1)} %get-tuple-element.48), kind=kOutput, calls=%fused_computation.32 | convolution fusion | flops 8594128896 | bytes 16777216 | tf_op jit(solution)/shard_map/dot_general | solution.py:93
  294.4 7.1 %collective-permute-done.11 = bf16[4,256,2048]{2,1,0:T(8,128)(2,1)} collective-permute-done((bf16[4,256,2048]{2,1,0:T(8,128)(2,1)}, bf16[4,256,2048]{2,1,0:T(8,128)(2,1)}, u32[]{:S(2)}, u32[]{:S(2)}) %collective-permute-start.11) | collective-permute-done | bytes 4194336 | tf_op jit(solution)/shard_map/ppermute | solution.py:96
  301.4 7.8 %fusion.9 = bf16[4,256,2048]{2,1,0:T(8,128)(2,1)} fusion(bf16[4,256,2048]{2,1,0:T(8,128)(2,1)} %collective-permute-done.11, bf16[4,2,256,2048]{3,2,1,0:T(8,128)(2,1)} %bitcast.215, s32[]{:T(128)S(6)} %select_n.24), kind=kLoop, calls=%fused_computation.14 | loop fusion | flops 8388608 | bytes 12582916 | tf_op jit(solution)/shard_map/convert_element_type | solution.py:99
  309.2 14.8 %fusion.16 = f32[1024,2048]{1,0:T(8,128)} fusion(bf16[1024,2048]{1,0:T(8,128)(2,1)} %copy-done.43, bf16[2048,4096]{1,0:T(8,128)(2,1)} %all-gather.8.cloned.1.call-done), kind=kOutput, calls=%fused_computation.36 | convolution fusion | flops 8589934592 | bytes 20971520 | tf_op jit(solution)/shard_map/dot_general | solution.py:239
  324.0 14.6 %multiply_convert_fusion = bf16[1024,2048]{1,0:T(8,128)(2,1)} fusion(f32[1024,2048]{1,0:T(8,128)} %get-tuple-element.50, bf16[1024,2048]{0,1:T(8,128)(2,1)S(1)} %copy-done.34, bf16[2048,4096]{1,0:T(8,128)(2,1)} %all-gather.8.cloned.1.call-done), kind=kOutput, calls=%fused_computation.20 | convolution fusion | flops 8594128896 | bytes 25165824 | tf_op jit(solution)/shard_map/dot_general | solution.py:236
  340.5 7.9 %add_convert_fusion.1 = bf16[1024,2048]{1,0:T(8,128)(2,1)} fusion(f32[1024,2048]{1,0:T(8,128)} %fusion.16, bf16[1024,512]{0,1:T(8,128)(2,1)S(1)} %bitcast.239, bf16[512,2048]{0,1:T(8,128)(2,1)S(1)} %bitcast.237), kind=kOutput, calls=%fused_computation.21 | convolution fusion | flops 2151677952 | bytes 15728640 | tf_op jit(solution)/shard_map/dot_general | solution.py:238
  348.4 10.4 %convolution_convert_fusion = bf16[2048,2048]{1,0:T(8,128)(2,1)S(1)} fusion(bf16[1024,2048]{1,0:T(8,128)(2,1)S(1)} %copy-done.42, bf16[1024,2048]{1,0:T(8,128)(2,1)S(1)} %copy-done.1, f32[2048]{0:T(1024)S(1)} %reshape.345, f32[2048]{0:T(1024)S(1)} %reshape.344, f32[1024]{0:T(1024)S(1)} %add_rsqrt_fusion, f32[1024]{0:T(1024)S(1)} %broadcast_multiply_fusion), kind=kOutput, calls=%fused_computation.31 | convolution fusion | flops 8606711808 | bytes 16801792 | tf_op jit(solution)/shard_map/dot_general | solution.py:93
  373.9 7.9 %fusion.8 = bf16[4,256,2048]{2,1,0:T(8,128)(2,1)} fusion(bf16[4,256,2048]{2,1,0:T(8,128)(2,1)} %collective-permute-done.15, bf16[4,2,256,2048]{3,2,1,0:T(8,128)(2,1)} %bitcast.213, s32[]{:T(128)S(6)} %select_n.24), kind=kLoop, calls=%fused_computation.12 | loop fusion | flops 8388608 | bytes 12582916 | tf_op jit(solution)/shard_map/convert_element_type | solution.py:99
  381.9 10.9 %fusion.70 = f32[1024,2048]{1,0:T(8,128)} fusion(bf16[1024,1536]{0,1:T(8,128)(2,1)S(1)} %bitcast.232, bf16[2048,1536]{1,0:T(8,128)(2,1)} %all-gather.6.cloned.1.call-done), kind=kOutput, calls=%fused_computation.176 | convolution fusion | flops 6442450944 | bytes 17825792 | tf_op jit(solution)/shard_map/dot_general | solution.py:253
  392.8 17.1 %add_convert_fusion = (bf16[1024,2048]{1,0:T(8,128)(2,1)}, f32[1024,2048]{1,0:T(8,128)}) fusion(f32[1024,2048]{1,0:T(8,128)} %fusion.70, f32[2048]{0:T(1024)S(1)} %reshape.344, f32[2048]{0:T(1024)S(1)} %reshape.342, bf16[1024,2048]{1,0:T(8,128)(2,1)} %multiply_convert_fusion, bf16[2048,4096]{1,0:T(8,128)(2,1)} %all-gather.8.cloned.1.call-done), kind=kOutput, calls=%fused_computation.17 | convolution fusion | flops 8598323200 | bytes 33570816 | tf_op jit(solution)/shard_map/dot_general | solution.py:252
  409.9 9.5 %collective-permute-done.13 = bf16[256,2048]{1,0:T(8,128)(2,1)} collective-permute-done((bf16[256,2048]{1,0:T(8,128)(2,1)}, bf16[256,2048]{1,0:T(8,128)(2,1)}, u32[]{:S(2)}, u32[]{:S(2)}) %collective-permute-start.13) | collective-permute-done | bytes 1048608 | tf_op jit(solution)/shard_map/ppermute | solution.py:24
  419.5 9.3 %multiply_reduce_fusion.1 = (f32[2048]{0:T(1024)S(1)}, f32[2048]{0:T(1024)S(1)}, f32[2048]{0:T(1024)S(1)}, f32[2048]{0:T(1024)S(1)}, f32[1024,2048]{1,0:T(8,128)}) fusion(f32[1024,2048]{1,0:T(8,128)S(1)} %copy-done.7, bf16[1024,2048]{1,0:T(8,128)(2,1)S(1)} %copy-done.2, f32[1024]{0:T(1024)S(1)} %add_rsqrt_fusion, f32[1024]{0:T(1024)S(1)} %broadcast_multiply_fusion, ...), kind=kLoop, calls=%fused_computation.16 | loop fusion | flops 18866176 | bytes 29401088 | tf_op jit(solution)/shard_map/reduce_sum | solution.py:258
  429.9 5.1 all-to-all-start.2
  444.7 4.2 all-to-all-start.3
  456.7 5.0 all-to-all-done.3
  473.0 11.5 %collective-permute-done.18 = bf16[256,2048]{1,0:T(8,128)(2,1)S(1)} collective-permute-done((bf16[256,2048]{1,0:T(8,128)(2,1)}, bf16[256,2048]{1,0:T(8,128)(2,1)S(1)}, u32[]{:S(2)}, u32[]{:S(2)}) %collective-permute-start.18) | collective-permute-done | bytes 1048608 | tf_op jit(solution)/shard_map/ppermute | solution.py:24
  484.5 20.8 %collective-permute-done.17 = bf16[256,2048]{1,0:T(8,128)(2,1)S(1)} collective-permute-done((bf16[256,2048]{1,0:T(8,128)(2,1)}, bf16[256,2048]{1,0:T(8,128)(2,1)S(1)}, u32[]{:S(2)}, u32[]{:S(2)}) %collective-permute-start.17) | collective-permute-done | bytes 1048608 | tf_op jit(solution)/shard_map/ppermute | solution.py:24
  509.5 4.3 all-to-all-start.5
  519.4 8.3 %all-to-all-done.5 = bf16[4,64,2048]{2,1,0:T(8,128)(2,1)} async-done(((bf16[4,64,2048]{2,1,0:T(8,128)(2,1)}), bf16[4,64,2048]{2,1,0:T(8,128)(2,1)}, u32[]{:S(2)}, u32[]{:S(2)}) %all-to-all-start.5) | async-done | bytes 1048608 | tf_op jit(solution)/shard_map/all_to_all | solution.py:121
  535.9 12.0 %all-to-all-done.4 = bf16[4,64,2048]{2,1,0:T(8,128)(2,1)S(1)} async-done(((bf16[4,64,2048]{2,1,0:T(8,128)(2,1)}), bf16[4,64,2048]{2,1,0:T(8,128)(2,1)S(1)}, u32[]{:S(2)}, u32[]{:S(2)}) %all-to-all-start.4) | async-done | bytes 1048608 | tf_op jit(solution)/shard_map/all_to_all | solution.py:121
  (267 shorter events, 179.4 us)
Async XLA Ops:
  7.2 119.8 %all-gather.4.cloned.1.call-start = ((), (), s32[]{:S(2)}) async-start(), calls=%async_computation.9 | async-start | bytes 2359296 | tf_op jit(solution)/shard_map/all_gather | solution.py:88
  7.9 126.7 %all-gather.6.cloned.1.call-start = ((), (), s32[]{:S(2)}) async-start(), calls=%async_computation.10 | async-start | bytes 7077888 | tf_op jit(solution)/shard_map/all_gather | solution.py:88
  28.3 232.4 %all-gather.8.cloned.1.call-start = ((), (), s32[]{:S(2)}) async-start(), calls=%async_computation.11 | async-start | bytes 18874368 | tf_op jit(solution)/shard_map/all_gather | solution.py:88
  41.2 27.9 %copy-start.27 = (bf16[1,256,2048]{2,1,0:T(8,128)(2,1)S(1)}, bf16[1,256,2048]{2,1,0:T(8,128)(2,1)}, u32[]{:S(2)}) copy-start(bf16[1,256,2048]{2,1,0:T(8,128)(2,1)} %param.12) | copy-start | bytes 3145732
  68.7 313.2 %reduce-scatter.4.cloned.1.call-start = ((), (), s32[]{:S(2)}) async-start(), calls=%async_computation.12 | async-start | bytes 5242880 | tf_op jit(solution)/shard_map/reduce_scatter | solution.py:103
  72.2 111.7 %copy-start.5 = (bf16[256,8,4,64]{0,3,2,1:T(8,128)(2,1)}, bf16[256,8,4,64]{0,3,2,1:T(8,128)(2,1)S(1)}, u32[]{:S(2)}) copy-start(bf16[256,8,4,64]{0,3,2,1:T(8,128)(2,1)S(1)} %copy.142) | copy-start | bytes 3145732
  72.2 6.7 %collective-permute-start.3 = (s32[1,2,256]{2,1,0:T(2,128)S(1)}, s32[1,2,256]{2,1,0:T(2,128)S(1)}, u32[]{:S(2)}, u32[]{:S(2)}) collective-permute-start(s32[1,2,256]{2,1,0:T(2,128)S(1)} %add_bitcast_fusion), channel_id=1, source_target_pairs={{0,8},{8,0},{16,24},{24,16},{1,9},{9,1},{17,25},{25,17},{2,10},{10... | collective-permute-start | bytes 6152 | tf_op jit(solution)/shard_map/ppermute | solution.py:24
  73.2 21.1 %collective-permute-start.5 = (s32[1,2,256]{2,1,0:T(2,128)S(1)}, s32[1,2,256]{2,1,0:T(2,128)S(1)}, u32[]{:S(2)}, u32[]{:S(2)}) collective-permute-start(s32[1,2,256]{2,1,0:T(2,128)S(1)} %add_bitcast_fusion), channel_id=1, source_target_pairs={{0,24},{8,16},{16,8},{24,0},{1,25},{9,17},{17,9},{25,1},{2,26},{10... | collective-permute-start | bytes 6152 | tf_op jit(solution)/shard_map/ppermute | solution.py:24
  74.7 19.6 %collective-permute-start.4 = (s32[1,2,256]{2,1,0:T(2,128)S(1)}, s32[1,2,256]{2,1,0:T(2,128)S(1)}, u32[]{:S(2)}, u32[]{:S(2)}) collective-permute-start(s32[1,2,256]{2,1,0:T(2,128)S(1)} %add_bitcast_fusion), channel_id=1, source_target_pairs={{0,16},{8,24},{16,0},{24,8},{1,17},{9,25},{17,1},{25,9},{2,18},{10... | collective-permute-start | bytes 6152 | tf_op jit(solution)/shard_map/ppermute | solution.py:24
  76.4 27.0 %collective-permute-start.2 = (bf16[256,2048]{1,0:T(8,128)(2,1)S(1)}, bf16[256,2048]{1,0:T(8,128)(2,1)S(1)}, u32[]{:S(2)}, u32[]{:S(2)}) collective-permute-start(bf16[256,2048]{1,0:T(8,128)(2,1)S(1)} %copy.130), channel_id=1, source_target_pairs={{0,24},{8,16},{16,8},{24,0},{1,25},{9,17},{17,9},{25,1},{2,26},{10... | collective-permute-start | bytes 3145736 | tf_op jit(solution)/shard_map/ppermute | solution.py:24
  77.4 43.8 %collective-permute-start.1 = (bf16[256,2048]{1,0:T(8,128)(2,1)S(1)}, bf16[256,2048]{1,0:T(8,128)(2,1)S(1)}, u32[]{:S(2)}, u32[]{:S(2)}) collective-permute-start(bf16[256,2048]{1,0:T(8,128)(2,1)S(1)} %copy.130), channel_id=1, source_target_pairs={{0,16},{8,24},{16,0},{24,8},{1,17},{9,25},{17,1},{25,9},{2,18},{10... | collective-permute-start | bytes 3145736 | tf_op jit(solution)/shard_map/ppermute | solution.py:24
  78.9 42.3 %collective-permute-start = (bf16[256,2048]{1,0:T(8,128)(2,1)S(1)}, bf16[256,2048]{1,0:T(8,128)(2,1)S(1)}, u32[]{:S(2)}, u32[]{:S(2)}) collective-permute-start(bf16[256,2048]{1,0:T(8,128)(2,1)S(1)} %copy.130), channel_id=1, source_target_pairs={{0,8},{8,0},{16,24},{24,16},{1,9},{9,1},{17,25},{25,17},{2,10},{10... | collective-permute-start | bytes 3145736 | tf_op jit(solution)/shard_map/ppermute | solution.py:24
  123.5 31.8 %collective-permute-start.8 = (bf16[256,2048]{0,1:T(8,128)(2,1)S(1)}, bf16[256,2048]{0,1:T(8,128)(2,1)}, u32[]{:S(2)}, u32[]{:S(2)}) collective-permute-start(bf16[256,2048]{0,1:T(8,128)(2,1)S(1)} %bitcast.205), channel_id=1, source_target_pairs={{0,24},{8,16},{16,8},{24,0},{1,25},{9,17},{17,9},{25,1},{2,26},{10... | collective-permute-start | bytes 3145736 | tf_op jit(solution)/shard_map/ppermute | solution.py:24
  124.8 47.3 %collective-permute-start.7 = (bf16[256,2048]{0,1:T(8,128)(2,1)S(1)}, bf16[256,2048]{0,1:T(8,128)(2,1)}, u32[]{:S(2)}, u32[]{:S(2)}) collective-permute-start(bf16[256,2048]{0,1:T(8,128)(2,1)S(1)} %bitcast.206), channel_id=1, source_target_pairs={{0,16},{8,24},{16,0},{24,8},{1,17},{9,25},{17,1},{25,9},{2,18},{10... | collective-permute-start | bytes 3145736 | tf_op jit(solution)/shard_map/ppermute | solution.py:24
  126.2 45.9 %collective-permute-start.6 = (bf16[256,2048]{0,1:T(8,128)(2,1)S(1)}, bf16[256,2048]{0,1:T(8,128)(2,1)}, u32[]{:S(2)}, u32[]{:S(2)}) collective-permute-start(bf16[256,2048]{0,1:T(8,128)(2,1)S(1)} %bitcast.207), channel_id=1, source_target_pairs={{0,8},{8,0},{16,24},{24,16},{1,9},{9,1},{17,25},{25,17},{2,10},{10... | collective-permute-start | bytes 3145736 | tf_op jit(solution)/shard_map/ppermute | solution.py:24
  134.6 284.8 %copy-start.35 = (f32[1024]{0:T(1024)}, f32[1024]{0:T(1024)S(1)}, u32[]{:S(2)}) copy-start(f32[1024]{0:T(1024)S(1)} %add_rsqrt_fusion) | copy-start | bytes 12292
  239.9 14.3 %collective-permute-start.9 = (bf16[4,256,1536]{2,1,0:T(8,128)(2,1)S(1)}, bf16[4,256,1536]{2,1,0:T(8,128)(2,1)}, u32[]{:S(2)}, u32[]{:S(2)}) collective-permute-start(bf16[4,256,1536]{2,1,0:T(8,128)(2,1)S(1)} %dynamic-slice_bitcast_fusion.2), channel_id=1, source_target_pairs={{0,1},{1,0},{2,3},{3,2},{4,5},{5,4},{6,7},{7,6},{8,9},{9,8},{10,11... | collective-permute-start | bytes 9437192 | tf_op jit(solution)/shard_map/ppermute | solution.py:96
  249.2 3.0 collective-permute-start.10
  293.9 7.5 %collective-permute-start.11 = (bf16[4,256,2048]{2,1,0:T(8,128)(2,1)}, bf16[4,256,2048]{2,1,0:T(8,128)(2,1)}, u32[]{:S(2)}, u32[]{:S(2)}) collective-permute-start(bf16[4,256,2048]{2,1,0:T(8,128)(2,1)} %dynamic-slice_bitcast_fusion.1), channel_id=1, source_target_pairs={{0,1},{1,0},{2,3},{3,2},{4,5},{5,4},{6,7},{7,6},{8,9},{9,8},{10,11... | collective-permute-start | bytes 12582920 | tf_op jit(solution)/shard_map/ppermute | solution.py:96
  294.3 215.2 %reduce-scatter.8.cloned.1.call-start = ((), (), s32[]{:S(2)}) async-start(), calls=%async_computation.14 | async-start | bytes 5242880 | tf_op jit(solution)/shard_map/reduce_scatter | solution.py:103
  338.6 192.2 %reduce-scatter.6.cloned.1.call-start = ((), (), s32[]{:S(2)}) async-start(), calls=%async_computation.13 | async-start | bytes 5242880 | tf_op jit(solution)/shard_map/reduce_scatter | solution.py:103
  363.7 10.2 %collective-permute-start.15 = (bf16[4,256,2048]{2,1,0:T(8,128)(2,1)}, bf16[4,256,2048]{2,1,0:T(8,128)(2,1)}, u32[]{:S(2)}, u32[]{:S(2)}) collective-permute-start(bf16[4,256,2048]{2,1,0:T(8,128)(2,1)} %dynamic-slice_bitcast_fusion), channel_id=1, source_target_pairs={{0,1},{1,0},{2,3},{3,2},{4,5},{5,4},{6,7},{7,6},{8,9},{9,8},{10,11... | collective-permute-start | bytes 12582920 | tf_op jit(solution)/shard_map/ppermute | solution.py:96
  370.4 39.5 %collective-permute-start.14 = (bf16[256,2048]{1,0:T(8,128)(2,1)}, bf16[256,2048]{1,0:T(8,128)(2,1)}, u32[]{:S(2)}, u32[]{:S(2)}) collective-permute-start(bf16[256,2048]{1,0:T(8,128)(2,1)} %get-tuple-element.110), channel_id=1, source_target_pairs={{0,24},{8,16},{16,8},{24,0},{1,25},{9,17},{17,9},{25,1},{2,26},{10... | collective-permute-start | bytes 3145736 | tf_op jit(solution)/shard_map/ppermute | solution.py:24
  372.3 47.1 %collective-permute-start.13 = (bf16[256,2048]{1,0:T(8,128)(2,1)}, bf16[256,2048]{1,0:T(8,128)(2,1)}, u32[]{:S(2)}, u32[]{:S(2)}) collective-permute-start(bf16[256,2048]{1,0:T(8,128)(2,1)} %get-tuple-element.111), channel_id=1, source_target_pairs={{0,16},{8,24},{16,0},{24,8},{1,17},{9,25},{17,1},{25,9},{2,18},{10... | collective-permute-start | bytes 3145736 | tf_op jit(solution)/shard_map/ppermute | solution.py:24
  373.2 46.2 %collective-permute-start.12 = (bf16[256,2048]{1,0:T(8,128)(2,1)}, bf16[256,2048]{1,0:T(8,128)(2,1)}, u32[]{:S(2)}, u32[]{:S(2)}) collective-permute-start(bf16[256,2048]{1,0:T(8,128)(2,1)} %get-tuple-element.112), channel_id=1, source_target_pairs={{0,8},{8,0},{16,24},{24,16},{1,9},{9,1},{17,25},{25,17},{2,10},{10... | collective-permute-start | bytes 3145736 | tf_op jit(solution)/shard_map/ppermute | solution.py:24
  429.9 14.8 %all-to-all-start.2 = ((f32[32,1,256]{2,1,0:T(1,128)}), f32[32,1,256]{2,1,0:T(1,128)S(1)}, u32[]{:S(2)}, u32[]{:S(2)}) async-start(f32[32,1,256]{2,1,0:T(1,128)} %all_to_all.28), calls=%async_computation.3 | async-start | bytes 65536 | tf_op jit(solution)/shard_map/all_to_all | solution.py:267
  444.7 17.0 %all-to-all-start.3 = ((bf16[4,64,1536]{2,1,0:T(8,128)(2,1)}), bf16[4,64,1536]{2,1,0:T(8,128)(2,1)}, u32[]{:S(2)}, u32[]{:S(2)}) async-start(bf16[4,64,1536]{2,1,0:T(8,128)(2,1)} %bitcast.58), calls=%async_computation.4 | async-start | bytes 1572864 | tf_op jit(solution)/shard_map/all_to_all | solution.py:121
  452.5 32.0 %collective-permute-start.18 = (bf16[256,2048]{1,0:T(8,128)(2,1)}, bf16[256,2048]{1,0:T(8,128)(2,1)S(1)}, u32[]{:S(2)}, u32[]{:S(2)}) collective-permute-start(bf16[256,2048]{1,0:T(8,128)(2,1)} %get-tuple-element.107), channel_id=1, source_target_pairs={{0,24},{8,16},{16,8},{24,0},{1,25},{9,17},{17,9},{25,1},{2,26},{10... | collective-permute-start | bytes 3145736 | tf_op jit(solution)/shard_map/ppermute | solution.py:24
  455.4 49.9 %collective-permute-start.17 = (bf16[256,2048]{1,0:T(8,128)(2,1)}, bf16[256,2048]{1,0:T(8,128)(2,1)S(1)}, u32[]{:S(2)}, u32[]{:S(2)}) collective-permute-start(bf16[256,2048]{1,0:T(8,128)(2,1)} %get-tuple-element.108), channel_id=1, source_target_pairs={{0,16},{8,24},{16,0},{24,8},{1,17},{9,25},{17,1},{25,9},{2,18},{10... | collective-permute-start | bytes 3145736 | tf_op jit(solution)/shard_map/ppermute | solution.py:24
  456.0 49.4 %collective-permute-start.16 = (bf16[256,2048]{1,0:T(8,128)(2,1)}, bf16[256,2048]{1,0:T(8,128)(2,1)S(1)}, u32[]{:S(2)}, u32[]{:S(2)}) collective-permute-start(bf16[256,2048]{1,0:T(8,128)(2,1)} %get-tuple-element.109), channel_id=1, source_target_pairs={{0,8},{8,0},{16,24},{24,16},{1,9},{9,1},{17,25},{25,17},{2,10},{10... | collective-permute-start | bytes 3145736 | tf_op jit(solution)/shard_map/ppermute | solution.py:24
  509.5 18.2 %all-to-all-start.5 = ((bf16[4,64,2048]{2,1,0:T(8,128)(2,1)}), bf16[4,64,2048]{2,1,0:T(8,128)(2,1)}, u32[]{:S(2)}, u32[]{:S(2)}) async-start(bf16[4,64,2048]{2,1,0:T(8,128)(2,1)} %bitcast.241), calls=%async_computation.8 | async-start | bytes 2097152 | tf_op jit(solution)/shard_map/all_to_all | solution.py:121
  530.8 17.1 %all-to-all-start.4 = ((bf16[4,64,2048]{2,1,0:T(8,128)(2,1)}), bf16[4,64,2048]{2,1,0:T(8,128)(2,1)S(1)}, u32[]{:S(2)}, u32[]{:S(2)}) async-start(bf16[4,64,2048]{2,1,0:T(8,128)(2,1)} %bitcast.242), calls=%async_computation.6 | async-start | bytes 2097152 | tf_op jit(solution)/shard_map/all_to_all | solution.py:121
  (42 other events, 340.4 us)
Sparse Core Ops, SparseCore 0:
  9.6 31.8 all-gather.3
  43.1 64.0 all-gather.5
  108.9 149.7 all-gather.7
  294.4 76.8 reduce-scatter.3
  373.5 77.8 reduce-scatter.7
  453.5 77.2 reduce-scatter.5

commit v2 on v1

--- a/solution.py
+++ b/solution.py
@@ -115,12 +115,27 @@
     return jnp.swapaxes(split, 1, 2).reshape(rows // count, columns * count)
 
 
-def return_columns(summed, groups):
-    count = lax.axis_size("ctx")
-    rows, columns = summed.shape[0] // count, summed.shape[1]
-    mine = lax.all_to_all(summed.reshape(count, rows, columns), "ctx", 0, 0, tiled=True)
-    part = columns // groups
-    pieces = [mine[c, :, g * part : (g + 1) * part] for g in range(groups) for c in range(count)]
+def return_columns(summed, groups, until):
+    count = lax.axis_size("ctx")
+    split = summed.reshape(count, summed.shape[0] // count, summed.shape[1])
+    mine = lax.all_to_all(split, "ctx", 0, 0, tiled=True)
+    return row_shard(after(mine, until), groups)
+
+
+def return_early(pair):
+    count, lines = lax.axis_size("ctx"), lax.axis_size("line")
+    split = pair.reshape(lines, count, -1, pair.shape[1]).swapaxes(0, 1)
+    return lax.all_to_all(split, "ctx", 0, 0, tiled=True)
+
+
+def row_shard(mine, groups):
+    if groups > 1:
+        split = mine.reshape(*mine.shape[:2], groups, -1).transpose(1, 2, 0, 3)
+        return split.reshape(mine.shape[1], -1).astype(jnp.float32)
+    part = mine.shape[2] // groups
+    pieces = [
+        mine[c, :, g * part : (g + 1) * part] for g in range(groups) for c in range(mine.shape[0])
+    ]
     return jnp.concatenate(pieces, 1).astype(jnp.float32)
 
 
@@ -178,7 +193,6 @@
     second_in = (normed * gain_two + bias_two).astype(bf16)
 
     projected = jnp.dot(first_in, qkv, preferred_element_type=f32)
-    grads = jnp.concatenate(after(grad_blocks, projected), 0)
     projected = projected.reshape(total_rows, 3, heads, HEAD_DIM)
     cosines, sines = rotary_tables(pos)
     queries = rotate(projected[:, 0], cosines, sines).astype(bf16)
@@ -195,6 +209,7 @@
     attended = jnp.einsum("hqk,khd->qhd", weights_low, values, preferred_element_type=f32)
     attended_low = attended.reshape(total_rows, heads * HEAD_DIM).astype(bf16)
 
+    grads = jnp.concatenate(after(grad_blocks, attended_low), 0)
     grad_attended = lax.dot_general(grads, out, COLS_BOTH, preferred_element_type=f32)
     grad_attended = grad_attended.reshape(total_rows, heads, HEAD_DIM)
     delta = jnp.sum(grad_attended * attended, axis=-1).T[..., None]
@@ -231,28 +246,27 @@
     slope = below + hidden_pre * bell
     activated, slope = lax.optimization_barrier((active, slope))
     pair_down = sum_pair(grads, activated)
-    summed_down = sum_rows(pair_down)
+    ready_down = return_early(pair_down)
     mlp = after(mlp, pair_down)
     grad_act = jnp.dot(grads, mlp[:, half:], preferred_element_type=f32)
     grad_hidden = (grad_act * slope).astype(bf16)
+    pair_up = sum_pair(second_in, grad_hidden)
+    summed_up = sum_rows(pair_up)
+    mlp, qkv, out = lax.optimization_barrier((mlp, qkv, out, pair_up))[:3]
     branches = jnp.dot(attended_low, out, preferred_element_type=f32)
     down_part = lax.dot_general(
         activated, mlp[:, half:], COLS_BOTH, preferred_element_type=f32
     )
     branches = (branches + down_part).astype(bf16)
-    grad_hidden = after(grad_hidden, branches)
-    pair_up = sum_pair(second_in, grad_hidden)
-    summed_up = sum_rows(pair_up)
-    output = scatter_ctx(branches, rows, pair_up) + own_tokens.astype(f32)
-    output = outer(output.astype(bf16))[None]
-
-    mlp, qkv, summed_attn = lax.optimization_barrier((mlp, qkv, summed_attn, pair_up))[:3]
-    summed_qkv = summed_attn[:, : qkv.shape[1]]
-    summed_out = unfold(summed_attn[:, qkv.shape[1] :], 1, ctx_count)
+    mlp, qkv = lax.optimization_barrier((mlp, qkv, branches))[:2]
     grad_second = lax.dot_general(grad_hidden, mlp[:, :half], COLS_BOTH, preferred_element_type=f32)
     grad_first = lax.dot_general(grad_projected, qkv, COLS_BOTH, preferred_element_type=f32)
     scaled = (grad_first * gain_one + grad_second * gain_two).astype(bf16)
     grad_first, grad_second, scaled = lax.optimization_barrier((grad_first, grad_second, scaled))
+    ready_down = after(ready_down, scaled).swapaxes(0, 1).reshape(pair_down.shape)
+    summed_down = sum_rows(ready_down)
+    output = scatter_ctx(branches, rows, ready_down) + own_tokens.astype(f32)
+    output = outer(output.astype(bf16))[None]
     norm_terms = jnp.stack(
         [
             jnp.sum(grad_first * normed, 0),
@@ -261,6 +275,10 @@
             jnp.sum(grad_second, 0),
         ]
     )
+    summed_attn = after(summed_attn, norm_terms)
+    summed_qkv = summed_attn[:, : mine_qkv.shape[1]]
+    summed_out = unfold(summed_attn[:, mine_qkv.shape[1] :], 1, ctx_count)
+    summed_up = after(summed_up, norm_terms)
     scaled = scatter_ctx(scaled, rows, norm_terms)
     norm_terms = norm_terms.reshape(4, fsdp_count, ctx_count, -1).transpose(2, 1, 0, 3)
     norm_terms = norm_terms.reshape(ctx_count * fsdp_count, -1)
@@ -279,10 +297,10 @@
         norm_sums[1],
         norm_sums[2],
         norm_sums[3],
-        return_columns(summed_qkv, 3),
+        return_columns(summed_qkv, 3, grad_tokens),
         outer(summed_out.astype(f32)),
-        return_columns(summed_up, 1),
-        return_columns(summed_down, 1),
+        return_columns(summed_up, 1, grad_tokens),
+        row_shard(summed_down.reshape(ctx_count, -1, summed_down.shape[1]), 1),
     )
 
 

time: 563 us -> 553 us (0.982)
  matrix products: 153 us -> 145 us
    ppermute x15, waiting for transfers between devices: 94.6 us -> 36.5 us  [swap(): return lax.ppermute(value, 'ctx', [(i, i ^ step) for i in range(count)])]
    all_to_all x1, waiting for transfers between devices: 0.01 us -> 26.8 us  [on_device(): norm_sums = lax.all_to_all(norm_terms, ('ctx', *FSDP), 0, 0, tiled=True)]
    all_to_all x3, waiting for transfers between devices: 25.3 us -> 46.2 us  [the longest x2 41.5 us: return_columns(): mine = lax.all_to_all(split, 'ctx', 0, 0, tiled=True)]
    unnamed x110 -> x89, local copies, waits for them, and re-layouts: 37.9 us -> 21.4 us
    all_gather x3, waiting for transfers between devices: 0.02 us -> 14.1 us  [gather_rows(): return lax.all_gather(mine, FSDP, axis=0, tiled=True)]
    convert_element_type x0 -> x3, local copies, waits for them, and re-layouts: none -> 8.2 us  [row_shard(): return split.reshape(mine.shape[1], -1).astype(jnp.float32)]
    convert_element_type x4, other arithmetic: 21.4 us -> 15.2 us  [sum_pair(): return pair.astype(jnp.bfloat16).reshape(-1, grad.shape[1])]
  transfers between devices with their start and end apart: 29 -> 29, of which waited for: 14 -> 9; matrix products, arithmetic and copies ran while one was open for 50% -> 56% of each run, Pallas kernels for 0% -> 0%
where the time goes in v2:
time: 553 us; the launch traced here: 547 us
  matrix products  145 us (26%)
  waiting for transfers between devices  130 us (24%)
  local copies, waits for them, and re-layouts  111 us (20%)
  other arithmetic  65.2 us (12%)
  blocking collectives  43.9 us (8%)
  starting transfers between devices  36.3 us (7%)
  between operations  15.6 us (3%)
    all_to_all x2, blocking collectives, exchange_columns(): mine = lax.all_to_all(split, 'ctx', 0, 0, tiled=True)  43.9 us
    all_to_all x2, waiting for transfers between devices, return_columns(): mine = lax.all_to_all(split, 'ctx', 0, 0, tiled=True)  41.5 us
    dot_general x4, matrix products, sum_pair(): lax.dot_general(left, right, ROWS_FIRST, preferred_element_type=jnp.float32)  37.5 us
    ppermute x15, waiting for transfers between devices, swap(): return lax.ppermute(value, 'ctx', [(i, i ^ step) for i in range(count)])  36.5 us
    all_to_all x1, waiting for transfers between devices, on_device(): norm_sums = lax.all_to_all(norm_terms, ('ctx', *FSDP), 0, 0, tiled=True)  26.8 us
    unnamed x89, local copies, waits for them, and re-layouts  21.4 us
    ppermute x15, starting transfers between devices, swap(): return lax.ppermute(value, 'ctx', [(i, i ^ step) for i in range(count)])  19.1 us
    dot_general x1, matrix products, on_device(): hidden_pre = jnp.dot(second_in, up, preferred_element_type=f32)  17.7 us
  transfers between devices with their start and end apart: 29, of which 9 were waited for; matrix products, arithmetic and copies ran while one was open for 56% of the time, Pallas kernels for 0%

profile of v2, /device:TPU:0, one launch (start us, length us, event | category | flops | bytes accessed | tf_op | source)
XLA Modules:
  0.0 547.3 jit_solution(8970529892586830777)
XLA Ops:
  11.8 16.4 %all_to_all.35 = bf16[4,64,1536]{2,1,0:T(8,128)(2,1)} all-to-all(bf16[4,64,1536]{2,1,0:T(8,128)(2,1)S(1)} %reshape.328), channel_id=1, replica_groups=mesh['ctx'=4,'line'=4,'core'=2] {'ctx'}, dimensions={0} | all-to-all | bytes 1572864 | tf_op jit(solution)/shard_map/all_to_all | solution.py:83
  41.2 27.5 %all_to_all.36 = bf16[4,64,4096]{2,1,0:T(8,128)(2,1)} all-to-all(bf16[4,64,4096]{2,1,0:T(8,128)(2,1)S(1)} %reshape.326), channel_id=1, replica_groups=mesh['ctx'=4,'line'=4,'core'=2] {'ctx'}, dimensions={0} | all-to-all | bytes 4194304 | tf_op jit(solution)/shard_map/all_to_all | solution.py:83
  80.4 14.5 %collective-permute-done.4 = s32[1,2,256]{2,1,0:T(2,128)S(1)} collective-permute-done((s32[1,2,256]{2,1,0:T(2,128)S(1)}, s32[1,2,256]{2,1,0:T(2,128)S(1)}, u32[]{:S(2)}, u32[]{:S(2)}) %collective-permute-start.4) | collective-permute-done | bytes 2080 | tf_op jit(solution)/shard_map/ppermute | solution.py:24
  99.9 4.1 collective-permute-done.2
  104.0 17.8 %collective-permute-done.1 = bf16[256,2048]{1,0:T(8,128)(2,1)S(1)} collective-permute-done((bf16[256,2048]{1,0:T(8,128)(2,1)}, bf16[256,2048]{1,0:T(8,128)(2,1)S(1)}, u32[]{:S(2)}, u32[]{:S(2)}) %collective-permute-start.1) | collective-permute-done | bytes 1048608 | tf_op jit(solution)/shard_map/ppermute | solution.py:24
  128.6 3.9 copy.178
  137.7 12.4 %fusion.50 = f32[1024,1536]{1,0:T(8,128)} fusion(bf16[2048,1536]{1,0:T(8,128)(2,1)} %all-gather.6.cloned.1.call-done, bf16[1024,2048]{1,0:T(8,128)(2,1)} %pad_maximum_fusion, f32[2048]{0:T(1024)S(1)} %reshape.355, f32[2048]{0:T(1024)S(1)} %reshape.354, f32[1024]{0:T(1024)S(1)} %add_rsqrt_fusion, f32[1024]{0:T(1024)S(1)} %broadcast_multiply_fusion), kind=kOutput, calls=%fused_computation.141 | convolution fusion | flops 6455033856 | bytes 16801792 | tf_op jit(solution)/shard_map/dot_general | solution.py:195
  150.1 8.1 %reshape.335 = f32[1024,3,2,256]{3,2,1,0:T(2,128)} reshape(f32[1024,1536]{1,0:T(8,128)} %fusion.50) | data formatting | bytes 12582912 | tf_op jit(solution)/shard_map/reshape | solution.py:196
  171.7 10.2 %fusion.57 = (f32[2,1024]{1,0:T(2,128)S(1)}, f32[2,1024,1024]{1,2,0:T(8,128)}) fusion(pred[1024,1024]{0,1:T(8,128)(4,1)} %compare_and_fusion, bf16[1024,2,192]{2,0,1:T(8,128)(2,1)S(1)} %slice.303, bf16[1024,2,64]{2,0,1:T(8,128)(2,1)} %get-tuple-element.152, bf16[1024,2,192]{2,0,1:T(8,128)(2,1)} %slice.304, bf16[1024,2,64]{2,0,1:T(8,128)(2,1)} %get-tuple-element.151), kind=kOutput, calls=%fused_computation.148 | convolution fusion | flops 1088422912 | bytes 11542528 | tf_op jit(solution)/shard_map/sub | solution.py:205
  181.8 4.9 fusion.25
  211.1 12.1 %convolution_convert_fusion.2 = bf16[2048,1536]{1,0:T(8,128)(2,1)S(1)} fusion(bf16[1024,1536]{0,1:T(8,128)(2,1)} %bitcast.189, bf16[1024,2048]{1,0:T(8,128)(2,1)} %pad_maximum_fusion, f32[2048]{0:T(1024)S(1)} %reshape.355, f32[2048]{0:T(1024)S(1)} %reshape.354, f32[1024]{0:T(1024)S(1)} %add_rsqrt_fusion, f32[1024]{0:T(1024)S(1)} %broadcast_multiply_fusion), kind=kOutput, calls=%fused_computation.37 | convolution fusion | flops 6458179584 | bytes 13656064 | tf_op jit(solution)/shard_map/dot_general | solution.py:93
  237.8 3.8 fusion.19
  244.5 14.1 %all-gather.8.cloned.1.call-done = bf16[2048,4096]{1,0:T(8,128)(2,1)} async-done(((bf16[256,4096]{1,0:T(8,128)(2,1)}), bf16[2048,4096]{1,0:T(8,128)(2,1)}) %all-gather.8.cloned.1.call-update) | async-done | bytes 16777232 | tf_op jit(solution)/shard_map/all_gather | solution.py:88
  258.6 17.7 %fusion.7 = (f32[1024,2048]{1,0:T(8,128)S(1)}, bf16[1024,2048]{1,0:T(8,128)(2,1)}) fusion(bf16[2048,4096]{1,0:T(8,128)(2,1)} %all-gather.8.cloned.1.call-done, bf16[1024,2048]{1,0:T(8,128)(2,1)} %pad_maximum_fusion, f32[2048]{0:T(1024)S(1)} %reshape.359, f32[2048]{0:T(1024)S(1)} %reshape.358, f32[1024]{0:T(1024)S(1)} %add_rsqrt_fusion, ...), kind=kOutput, calls=%fused_computation.10 | convolution fusion | flops 8623489024 | bytes 25190400 | tf_op jit(solution)/shard_map/dot_general | solution.py:242
  276.3 12.5 %multiply_convert_fusion = bf16[1024,2048]{1,0:T(8,128)(2,1)S(1)} fusion(f32[1024,2048]{1,0:T(8,128)S(1)} %get-tuple-element.53, bf16[1024,2048]{0,1:T(8,128)(2,1)S(1)} %copy-done.27, bf16[2048,4096]{1,0:T(8,128)(2,1)} %all-gather.8.cloned.1.call-done), kind=kOutput, calls=%fused_computation.25 | convolution fusion | flops 8594128896 | bytes 25165824 | tf_op jit(solution)/shard_map/dot_general | solution.py:251
  288.8 10.9 %convolution_convert_fusion.1 = bf16[2048,2048]{1,0:T(8,128)(2,1)S(1)} fusion(bf16[1024,2048]{1,0:T(8,128)(2,1)S(1)} %multiply_convert_fusion, bf16[1024,2048]{1,0:T(8,128)(2,1)S(1)} %copy-done.1, f32[2048]{0:T(1024)S(1)} %reshape.359, f32[2048]{0:T(1024)S(1)} %reshape.358, f32[1024]{0:T(1024)S(1)} %add_rsqrt_fusion, f32[1024]{0:T(1024)S(1)} %broadcast_multiply_fusion), kind=kOutput, calls=%fused_computation.36 | convolution fusion | flops 8606711808 | bytes 16801792 | tf_op jit(solution)/shard_map/dot_general | solution.py:93
  300.7 12.1 %convolution_convert_fusion = bf16[2048,2048]{1,0:T(8,128)(2,1)S(1)} fusion(bf16[1024,2048]{0,1:T(8,128)(2,1)} %copy-done.25, bf16[1024,2048]{1,0:T(8,128)(2,1)} %get-tuple-element.55), kind=kOutput, calls=%fused_computation.35 | convolution fusion | flops 8594128896 | bytes 16777216 | tf_op jit(solution)/shard_map/dot_general | solution.py:93
  317.6 4.1 fusion.11
  324.8 5.4 fusion.10
  332.5 4.8 all-to-all-start.2
  337.4 12.7 %fusion.14 = f32[1024,2048]{1,0:T(8,128)S(1)} fusion(bf16[1024,2048]{1,0:T(8,128)(2,1)} %get-tuple-element.55, bf16[2048,4096]{1,0:T(8,128)(2,1)} %all-gather.8.cloned.1.call-done), kind=kOutput, calls=%fused_computation.23 | convolution fusion | flops 8589934592 | bytes 20971520 | tf_op jit(solution)/shard_map/dot_general | solution.py:257
  350.2 4.5 add_convert_fusion.1
  354.7 9.0 %fusion.58 = f32[1024,2048]{1,0:T(8,128)S(1)} fusion(bf16[1024,1536]{0,1:T(8,128)(2,1)S(1)} %bitcast.190, bf16[2048,1536]{1,0:T(8,128)(2,1)} %all-gather.6.cloned.1.call-done), kind=kOutput, calls=%fused_computation.149 | convolution fusion | flops 6442450944 | bytes 17825792 | tf_op jit(solution)/shard_map/dot_general | solution.py:263
  363.7 17.2 %add_convert_fusion = (bf16[1024,2048]{1,0:T(8,128)(2,1)}, f32[1024,2048]{1,0:T(8,128)}) fusion(f32[1024,2048]{1,0:T(8,128)S(1)} %fusion.58, f32[2048]{0:T(1024)S(1)} %reshape.358, f32[2048]{0:T(1024)S(1)} %reshape.354, bf16[1024,2048]{1,0:T(8,128)(2,1)S(1)} %copy-done.36, bf16[2048,4096]{1,0:T(8,128)(2,1)} %all-gather.8.cloned.1.call-done), kind=kOutput, calls=%fused_computation.19 | convolution fusion | flops 8598323200 | bytes 33570816 | tf_op jit(solution)/shard_map/dot_general | solution.py:262
  380.9 4.7 all-to-all-done.2
  385.5 4.8 copy.205
  393.7 11.6 %multiply_reduce_fusion.1 = (f32[2048]{0:T(1024)S(1)}, f32[2048]{0:T(1024)S(1)}, f32[2048]{0:T(1024)S(1)}, f32[2048]{0:T(1024)S(1)}, f32[1024,2048]{1,0:T(8,128)}) fusion(f32[1024,2048]{1,0:T(8,128)} %copy-done.6, bf16[1024,2048]{1,0:T(8,128)(2,1)} %pad_maximum_fusion, f32[1024]{0:T(1024)S(1)} %add_rsqrt_fusion, f32[1024]{0:T(1024)S(1)} %broadcast_multiply_fusion, ...), kind=kLoop, calls=%fused_computation.18 | loop fusion | flops 18866176 | bytes 29401088 | tf_op jit(solution)/shard_map/reduce_sum | solution.py:272
  416.1 3.7 fusion.53
  432.5 26.8 %all-to-all-done.3 = f32[32,1,256]{2,1,0:T(1,128)S(1)} async-done(((f32[32,1,256]{2,1,0:T(1,128)}), f32[32,1,256]{2,1,0:T(1,128)S(1)}, u32[]{:S(2)}, u32[]{:S(2)}) %all-to-all-start.3) | async-done | bytes 32800 | tf_op jit(solution)/shard_map/all_to_all | solution.py:285
  459.3 4.2 all-to-all-start.4
  469.6 41.5 %all-to-all-done.4 = bf16[4,64,1536]{2,1,0:T(8,128)(2,1)} async-done(((bf16[4,64,1536]{2,1,0:T(8,128)(2,1)}), bf16[4,64,1536]{2,1,0:T(8,128)(2,1)}, u32[]{:S(2)}, u32[]{:S(2)}) %all-to-all-start.4) | async-done | bytes 786464 | tf_op jit(solution)/shard_map/all_to_all | solution.py:121
  511.1 4.5 all-to-all-start.5
  (251 shorter events, 169.2 us)
Async XLA Ops:
  7.2 121.4 %all-gather.4.cloned.1.call-start = ((), (), s32[]{:S(2)}) async-start(), calls=%async_computation.9 | async-start | bytes 2359296 | tf_op jit(solution)/shard_map/all_gather | solution.py:88
  7.9 129.8 %all-gather.6.cloned.1.call-start = ((), (), s32[]{:S(2)}) async-start(), calls=%async_computation.10 | async-start | bytes 7077888 | tf_op jit(solution)/shard_map/all_gather | solution.py:88
  28.3 230.4 %all-gather.8.cloned.1.call-start = ((), (), s32[]{:S(2)}) async-start(), calls=%async_computation.11 | async-start | bytes 18874368 | tf_op jit(solution)/shard_map/all_gather | solution.py:88
  68.7 344.0 %reduce-scatter.4.cloned.1.call-start = ((), (), s32[]{:S(2)}) async-start(), calls=%async_computation.12 | async-start | bytes 5242880 | tf_op jit(solution)/shard_map/reduce_scatter | solution.py:103
  71.9 117.1 %copy-start.4 = (bf16[256,8,4,64]{0,3,2,1:T(8,128)(2,1)}, bf16[256,8,4,64]{0,3,2,1:T(8,128)(2,1)S(1)}, u32[]{:S(2)}) copy-start(bf16[256,8,4,64]{0,3,2,1:T(8,128)(2,1)S(1)} %copy.187) | copy-start | bytes 3145732
  71.9 7.4 %collective-permute-start.3 = (s32[1,2,256]{2,1,0:T(2,128)S(1)}, s32[1,2,256]{2,1,0:T(2,128)S(1)}, u32[]{:S(2)}, u32[]{:S(2)}) collective-permute-start(s32[1,2,256]{2,1,0:T(2,128)S(1)} %add_bitcast_fusion), channel_id=1, source_target_pairs={{0,8},{8,0},{16,24},{24,16},{1,9},{9,1},{17,25},{25,17},{2,10},{10... | collective-permute-start | bytes 6152 | tf_op jit(solution)/shard_map/ppermute | solution.py:24
  72.9 22.0 %collective-permute-start.5 = (s32[1,2,256]{2,1,0:T(2,128)S(1)}, s32[1,2,256]{2,1,0:T(2,128)S(1)}, u32[]{:S(2)}, u32[]{:S(2)}) collective-permute-start(s32[1,2,256]{2,1,0:T(2,128)S(1)} %add_bitcast_fusion), channel_id=1, source_target_pairs={{0,24},{8,16},{16,8},{24,0},{1,25},{9,17},{17,9},{25,1},{2,26},{10... | collective-permute-start | bytes 6152 | tf_op jit(solution)/shard_map/ppermute | solution.py:24
  74.4 20.5 %collective-permute-start.4 = (s32[1,2,256]{2,1,0:T(2,128)S(1)}, s32[1,2,256]{2,1,0:T(2,128)S(1)}, u32[]{:S(2)}, u32[]{:S(2)}) collective-permute-start(s32[1,2,256]{2,1,0:T(2,128)S(1)} %add_bitcast_fusion), channel_id=1, source_target_pairs={{0,16},{8,24},{16,0},{24,8},{1,17},{9,25},{17,1},{25,9},{2,18},{10... | collective-permute-start | bytes 6152 | tf_op jit(solution)/shard_map/ppermute | solution.py:24
  76.9 27.1 %collective-permute-start.2 = (bf16[256,2048]{1,0:T(8,128)(2,1)}, bf16[256,2048]{1,0:T(8,128)(2,1)S(1)}, u32[]{:S(2)}, u32[]{:S(2)}) collective-permute-start(bf16[256,2048]{1,0:T(8,128)(2,1)} %copy.177), channel_id=1, source_target_pairs={{0,24},{8,16},{16,8},{24,0},{1,25},{9,17},{17,9},{25,1},{2,26},{10... | collective-permute-start | bytes 3145736 | tf_op jit(solution)/shard_map/ppermute | solution.py:24
  77.8 44.0 %collective-permute-start.1 = (bf16[256,2048]{1,0:T(8,128)(2,1)}, bf16[256,2048]{1,0:T(8,128)(2,1)S(1)}, u32[]{:S(2)}, u32[]{:S(2)}) collective-permute-start(bf16[256,2048]{1,0:T(8,128)(2,1)} %copy.177), channel_id=1, source_target_pairs={{0,16},{8,24},{16,0},{24,8},{1,17},{9,25},{17,1},{25,9},{2,18},{10... | collective-permute-start | bytes 3145736 | tf_op jit(solution)/shard_map/ppermute | solution.py:24
  79.3 42.6 %collective-permute-start = (bf16[256,2048]{1,0:T(8,128)(2,1)}, bf16[256,2048]{1,0:T(8,128)(2,1)S(1)}, u32[]{:S(2)}, u32[]{:S(2)}) collective-permute-start(bf16[256,2048]{1,0:T(8,128)(2,1)} %copy.177), channel_id=1, source_target_pairs={{0,8},{8,0},{16,24},{24,16},{1,9},{9,1},{17,25},{25,17},{2,10},{10... | collective-permute-start | bytes 3145736 | tf_op jit(solution)/shard_map/ppermute | solution.py:24
  125.1 63.9 %collective-permute-start.8 = (bf16[256,2048]{0,1:T(8,128)(2,1)S(1)}, bf16[256,2048]{0,1:T(8,128)(2,1)}, u32[]{:S(2)}, u32[]{:S(2)}) collective-permute-start(bf16[256,2048]{0,1:T(8,128)(2,1)S(1)} %bitcast.162), channel_id=1, source_target_pairs={{0,24},{8,16},{16,8},{24,0},{1,25},{9,17},{17,9},{25,1},{2,26},{10... | collective-permute-start | bytes 3145736 | tf_op jit(solution)/shard_map/ppermute | solution.py:24
  126.5 62.5 %collective-permute-start.7 = (bf16[256,2048]{0,1:T(8,128)(2,1)S(1)}, bf16[256,2048]{0,1:T(8,128)(2,1)}, u32[]{:S(2)}, u32[]{:S(2)}) collective-permute-start(bf16[256,2048]{0,1:T(8,128)(2,1)S(1)} %bitcast.163), channel_id=1, source_target_pairs={{0,16},{8,24},{16,0},{24,8},{1,17},{9,25},{17,1},{25,9},{2,18},{10... | collective-permute-start | bytes 3145736 | tf_op jit(solution)/shard_map/ppermute | solution.py:24
  127.9 61.1 %collective-permute-start.6 = (bf16[256,2048]{0,1:T(8,128)(2,1)S(1)}, bf16[256,2048]{0,1:T(8,128)(2,1)}, u32[]{:S(2)}, u32[]{:S(2)}) collective-permute-start(bf16[256,2048]{0,1:T(8,128)(2,1)S(1)} %bitcast.164), channel_id=1, source_target_pairs={{0,8},{8,0},{16,24},{24,16},{1,9},{9,1},{17,25},{25,17},{2,10},{10... | collective-permute-start | bytes 3145736 | tf_op jit(solution)/shard_map/ppermute | solution.py:24
  137.7 256.0 %copy-start.28 = (f32[1024]{0:T(1024)}, f32[1024]{0:T(1024)S(1)}, u32[]{:S(2)}) copy-start(f32[1024]{0:T(1024)S(1)} %add_rsqrt_fusion) | copy-start | bytes 12292
  223.5 14.3 %collective-permute-start.9 = (bf16[4,256,1536]{2,1,0:T(8,128)(2,1)S(1)}, bf16[4,256,1536]{2,1,0:T(8,128)(2,1)}, u32[]{:S(2)}, u32[]{:S(2)}) collective-permute-start(bf16[4,256,1536]{2,1,0:T(8,128)(2,1)S(1)} %dynamic-slice_bitcast_fusion.2), channel_id=1, source_target_pairs={{0,1},{1,0},{2,3},{3,2},{4,5},{5,4},{6,7},{7,6},{8,9},{9,8},{10,11... | collective-permute-start | bytes 9437192 | tf_op jit(solution)/shard_map/ppermute | solution.py:96
  232.8 3.0 collective-permute-start.10
  244.3 225.3 %reduce-scatter.6.cloned.1.call-start = ((), (), s32[]{:S(2)}) async-start(), calls=%async_computation.13 | async-start | bytes 5242880 | tf_op jit(solution)/shard_map/reduce_scatter | solution.py:103
  300.4 17.2 %collective-permute-start.11 = (bf16[4,256,2048]{2,1,0:T(8,128)(2,1)S(1)}, bf16[4,256,2048]{2,1,0:T(8,128)(2,1)S(1)}, u32[]{:S(2)}, u32[]{:S(2)}) collective-permute-start(bf16[4,256,2048]{2,1,0:T(8,128)(2,1)S(1)} %dynamic-slice_bitcast_fusion.1), channel_id=1, source_target_pairs={{0,1},{1,0},{2,3},{3,2},{4,5},{5,4},{6,7},{7,6},{8,9},{9,8},{10,11... | collective-permute-start | bytes 12582920 | tf_op jit(solution)/shard_map/ppermute | solution.py:96
  317.3 7.5 %collective-permute-start.15 = (bf16[4,256,2048]{2,1,0:T(8,128)(2,1)}, bf16[4,256,2048]{2,1,0:T(8,128)(2,1)}, u32[]{:S(2)}, u32[]{:S(2)}) collective-permute-start(bf16[4,256,2048]{2,1,0:T(8,128)(2,1)} %dynamic-slice_bitcast_fusion), channel_id=1, source_target_pairs={{0,1},{1,0},{2,3},{3,2},{4,5},{5,4},{6,7},{7,6},{8,9},{9,8},{10,11... | collective-permute-start | bytes 12582920 | tf_op jit(solution)/shard_map/ppermute | solution.py:96
  332.5 53.0 %all-to-all-start.2 = ((bf16[4,4,64,2048]{3,2,1,0:T(8,128)(2,1)}), bf16[4,4,64,2048]{3,2,1,0:T(8,128)(2,1)}, u32[]{:S(2)}, u32[]{:S(2)}) async-start(bf16[4,4,64,2048]{3,2,1,0:T(8,128)(2,1)} %copy.204), calls=%async_computation.2 | async-start | bytes 8388608 | tf_op jit(solution)/shard_map/all_to_all | solution.py:128
  337.4 199.9 %reduce-scatter.8.cloned.1.call-start = ((), (), s32[]{:S(2)}) async-start(), calls=%async_computation.14 | async-start | bytes 5242880 | tf_op jit(solution)/shard_map/reduce_scatter | solution.py:103
  409.2 55.0 %collective-permute-start.18 = (bf16[256,2048]{1,0:T(8,128)(2,1)}, bf16[256,2048]{1,0:T(8,128)(2,1)S(1)}, u32[]{:S(2)}, u32[]{:S(2)}) collective-permute-start(bf16[256,2048]{1,0:T(8,128)(2,1)} %get-tuple-element.127), channel_id=1, source_target_pairs={{0,24},{8,16},{16,8},{24,0},{1,25},{9,17},{17,9},{25,1},{2,26},{10... | collective-permute-start | bytes 3145736 | tf_op jit(solution)/shard_map/ppermute | solution.py:24
  410.6 55.5 %collective-permute-start.17 = (bf16[256,2048]{1,0:T(8,128)(2,1)}, bf16[256,2048]{1,0:T(8,128)(2,1)S(1)}, u32[]{:S(2)}, u32[]{:S(2)}) collective-permute-start(bf16[256,2048]{1,0:T(8,128)(2,1)} %get-tuple-element.128), channel_id=1, source_target_pairs={{0,16},{8,24},{16,0},{24,8},{1,17},{9,25},{17,1},{25,9},{2,18},{10... | collective-permute-start | bytes 3145736 | tf_op jit(solution)/shard_map/ppermute | solution.py:24
  412.1 54.1 %collective-permute-start.16 = (bf16[256,2048]{1,0:T(8,128)(2,1)}, bf16[256,2048]{1,0:T(8,128)(2,1)}, u32[]{:S(2)}, u32[]{:S(2)}) collective-permute-start(bf16[256,2048]{1,0:T(8,128)(2,1)} %get-tuple-element.129), channel_id=1, source_target_pairs={{0,8},{8,0},{16,24},{24,16},{1,9},{9,1},{17,25},{25,17},{2,10},{10... | collective-permute-start | bytes 3145736 | tf_op jit(solution)/shard_map/ppermute | solution.py:24
  413.5 45.8 %all-to-all-start.3 = ((f32[32,1,256]{2,1,0:T(1,128)}), f32[32,1,256]{2,1,0:T(1,128)S(1)}, u32[]{:S(2)}, u32[]{:S(2)}) async-start(f32[32,1,256]{2,1,0:T(1,128)} %all_to_all.28), calls=%async_computation.3 | async-start | bytes 65536 | tf_op jit(solution)/shard_map/all_to_all | solution.py:285
  429.4 100.0 %collective-permute-start.14 = (bf16[256,2048]{1,0:T(8,128)(2,1)}, bf16[256,2048]{1,0:T(8,128)(2,1)}, u32[]{:S(2)}, u32[]{:S(2)}) collective-permute-start(bf16[256,2048]{1,0:T(8,128)(2,1)} %get-tuple-element.130), channel_id=1, source_target_pairs={{0,24},{8,16},{16,8},{24,0},{1,25},{9,17},{17,9},{25,1},{2,26},{10... | collective-permute-start | bytes 3145736 | tf_op jit(solution)/shard_map/ppermute | solution.py:24
  432.0 97.4 %collective-permute-start.13 = (bf16[256,2048]{1,0:T(8,128)(2,1)}, bf16[256,2048]{1,0:T(8,128)(2,1)}, u32[]{:S(2)}, u32[]{:S(2)}) collective-permute-start(bf16[256,2048]{1,0:T(8,128)(2,1)} %get-tuple-element.131), channel_id=1, source_target_pairs={{0,16},{8,24},{16,0},{24,8},{1,17},{9,25},{17,1},{25,9},{2,18},{10... | collective-permute-start | bytes 3145736 | tf_op jit(solution)/shard_map/ppermute | solution.py:24
  459.3 51.8 %all-to-all-start.4 = ((bf16[4,64,1536]{2,1,0:T(8,128)(2,1)}), bf16[4,64,1536]{2,1,0:T(8,128)(2,1)}, u32[]{:S(2)}, u32[]{:S(2)}) async-start(bf16[4,64,1536]{2,1,0:T(8,128)(2,1)} %bitcast.192), calls=%async_computation.5 | async-start | bytes 1572864 | tf_op jit(solution)/shard_map/all_to_all | solution.py:121
  464.2 65.2 %collective-permute-start.12 = (bf16[256,2048]{1,0:T(8,128)(2,1)}, bf16[256,2048]{1,0:T(8,128)(2,1)}, u32[]{:S(2)}, u32[]{:S(2)}) collective-permute-start(bf16[256,2048]{1,0:T(8,128)(2,1)} %get-tuple-element.132), channel_id=1, source_target_pairs={{0,8},{8,0},{16,24},{24,16},{1,9},{9,1},{17,25},{25,17},{2,10},{10... | collective-permute-start | bytes 3145736 | tf_op jit(solution)/shard_map/ppermute | solution.py:24
  466.1 49.5 %slice-start.3 = ((f32[1024]{0:T(1024)}), f32[256]{0:T(256)S(1)}, s32[]{:S(2)}) async-start(f32[1024]{0:T(1024)} %copy-done.28), calls=%async_computation.18 | async-start | bytes 2048 | tf_op jit(solution)/shard_map/slice | solution.py:291
  511.1 23.4 %all-to-all-start.5 = ((bf16[4,64,2048]{2,1,0:T(8,128)(2,1)}), bf16[4,64,2048]{2,1,0:T(8,128)(2,1)}, u32[]{:S(2)}, u32[]{:S(2)}) async-start(bf16[4,64,2048]{2,1,0:T(8,128)(2,1)} %bitcast.198), calls=%async_computation.7 | async-start | bytes 2097152 | tf_op jit(solution)/shard_map/all_to_all | solution.py:121
  (38 other events, 374.1 us)
Sparse Core Ops, SparseCore 0:
  9.6 31.8 all-gather.3
  43.1 64.0 all-gather.5
  108.9 149.7 all-gather.7
  260.8 74.9 reduce-scatter.3
  337.9 77.2 reduce-scatter.5
  417.4 77.2 reduce-scatter.7

commit v3 on v2

--- a/solution.py
+++ b/solution.py
@@ -86,6 +86,16 @@
 
 def gather_rows(mine):
     return lax.all_gather(mine, FSDP, axis=0, tiled=True)
+
+
+def gather_small(mine):
+    lines, core, line = lax.axis_size("line"), lax.axis_index("core"), lax.axis_index("line")
+    came = [lax.ppermute(mine, "line", [(i, i ^ k) for i in range(lines)]) for k in range(1, lines)]
+    same = jnp.stack([mine, *came])
+    other = lax.ppermute(same, "core", [(0, 1), (1, 0)])
+    both = jnp.stack([jnp.where(core == 0, same, other), jnp.where(core == 0, other, same)], 1)
+    rows = [lax.dynamic_index_in_dim(both, line ^ k, 0, keepdims=False) for k in range(lines)]
+    return jnp.stack(rows).reshape(-1, mine.shape[1])
 
 
 def sum_pair(left, right):
@@ -168,7 +178,7 @@
     def outer(value):
         return turn(value, fsdp_count, ctx_count)
 
-    out = inner(gather_rows(w_out))
+    out = inner(gather_small(w_out))
     mine_qkv = exchange_columns(w_qkv, 3)
     qkv = gather_rows(mine_qkv)
     mine_mlp = exchange_columns(jnp.concatenate([w_up, w_down], 1), 2, mine_qkv)

time: 553 us -> 595 us (1.076)
  waiting for transfers between devices: 130 us -> 159 us
  local copies, waits for them, and re-layouts: 111 us -> 118 us
    ppermute x0 -> x4, waiting for transfers between devices: none -> 40.4 us  [the longest x3 40.4 us: gather_small(): lax.ppermute(mine, 'line', [(i, i ^ k) for i in range(lines)])]
    all_gather x3 -> x2, waiting for transfers between devices: 14.1 us -> 0.04 us  [gather_rows(): return lax.all_gather(mine, FSDP, axis=0, tiled=True)]
    another operation x0 -> x2, local copies, waits for them, and re-layouts: none -> 8.69 us  [the longest x1 7.23 us: turn(): split = value.reshape(*lead, first, second, width // (first * second))]
    unnamed x89 -> x97, local copies, waits for them, and re-layouts: 21.4 us -> 21.7 us
  transfers between devices with their start and end apart: 29 -> 32, of which waited for: 9 -> 10; matrix products, arithmetic and copies ran while one was open for 56% -> 53% of each run, Pallas kernels for 0% -> 0%
where the time goes in v3:
time: 595 us; the launch traced here: 588 us
  waiting for transfers between devices  159 us (27%)
  matrix products  146 us (25%)
  local copies, waits for them, and re-layouts  118 us (20%)
  other arithmetic  65.9 us (11%)
  blocking collectives  44.1 us (7%)
  starting transfers between devices  40.7 us (7%)
  between operations  15.2 us (3%)
    all_to_all x2, blocking collectives, exchange_columns(): mine = lax.all_to_all(split, 'ctx', 0, 0, tiled=True)  44.1 us
    all_to_all x2, waiting for transfers between devices, return_columns(): mine = lax.all_to_all(split, 'ctx', 0, 0, tiled=True)  41.5 us
    ppermute x3, waiting for transfers between devices, gather_small(): lax.ppermute(mine, 'line', [(i, i ^ k) for i in range(lines)])  40.4 us
    ppermute x15, waiting for transfers between devices, swap(): return lax.ppermute(value, 'ctx', [(i, i ^ step) for i in range(count)])  39.7 us
    dot_general x4, matrix products, sum_pair(): lax.dot_general(left, right, ROWS_FIRST, preferred_element_type=jnp.float32)  37.8 us
    all_to_all x1, waiting for transfers between devices, on_device(): norm_sums = lax.all_to_all(norm_terms, ('ctx', *FSDP), 0, 0, tiled=True)  26.8 us
    unnamed x97, local copies, waits for them, and re-layouts  21.7 us
    ppermute x15, starting transfers between devices, swap(): return lax.ppermute(value, 'ctx', [(i, i ^ step) for i in range(count)])  19.2 us
  transfers between devices with their start and end apart: 32, of which 10 were waited for; matrix products, arithmetic and copies ran while one was open for 53% of the time, Pallas kernels for 0%

profile of v3, /device:TPU:0, one launch (start us, length us, event | category | flops | bytes accessed | tf_op | source)
XLA Modules:
  0.0 588.4 jit_solution(17501205102503238588)
XLA Ops:
  11.2 16.4 %all_to_all.35 = bf16[4,64,1536]{2,1,0:T(8,128)(2,1)} all-to-all(bf16[4,64,1536]{2,1,0:T(8,128)(2,1)S(1)} %reshape.325), channel_id=1, replica_groups=mesh['ctx'=4,'line'=4,'core'=2] {'ctx'}, dimensions={0} | all-to-all | bytes 1572864 | tf_op jit(solution)/shard_map/all_to_all | solution.py:83
  40.5 27.6 %all_to_all.36 = bf16[4,64,4096]{2,1,0:T(8,128)(2,1)} all-to-all(bf16[4,64,4096]{2,1,0:T(8,128)(2,1)S(1)} %reshape.323), channel_id=1, replica_groups=mesh['ctx'=4,'line'=4,'core'=2] {'ctx'}, dimensions={0} | all-to-all | bytes 4194304 | tf_op jit(solution)/shard_map/all_to_all | solution.py:83
  72.4 21.1 %collective-permute-done.3 = bf16[64,2048]{1,0:T(8,128)(2,1)S(1)} collective-permute-done((bf16[64,2048]{1,0:T(8,128)(2,1)S(1)}, bf16[64,2048]{1,0:T(8,128)(2,1)S(1)}, u32[]{:S(2)}, u32[]{:S(2)}) %collective-permute-start.3) | collective-permute-done | bytes 262176 | tf_op jit(solution)/shard_map/ppermute | solution.py:93
  96.3 16.6 %collective-permute-done.4 = bf16[64,2048]{1,0:T(8,128)(2,1)S(1)} collective-permute-done((bf16[64,2048]{1,0:T(8,128)(2,1)S(1)}, bf16[64,2048]{1,0:T(8,128)(2,1)S(1)}, u32[]{:S(2)}, u32[]{:S(2)}) %collective-permute-start.4) | collective-permute-done | bytes 262176 | tf_op jit(solution)/shard_map/ppermute | solution.py:93
  121.1 7.2 %reshape_reshape.9 = bf16[512,4,8,64]{3,2,1,0:T(8,128)(2,1)} reshape(bf16[4,2,64,2048]{3,2,1,0:T(8,128)(2,1)} %copy.178) | data formatting | bytes 4194304 | tf_op jit(solution)/shard_map/reshape;reshape | solution.py:44
  128.3 5.4 copy.179
  146.5 18.5 %collective-permute-done.2 = bf16[256,2048]{1,0:T(8,128)(2,1)S(1)} collective-permute-done((bf16[256,2048]{1,0:T(8,128)(2,1)S(1)}, bf16[256,2048]{1,0:T(8,128)(2,1)S(1)}, u32[]{:S(2)}, u32[]{:S(2)}) %collective-permute-start.2) | collective-permute-done | bytes 1048608 | tf_op jit(solution)/shard_map/ppermute | solution.py:24
  164.9 21.2 %collective-permute-done.1 = bf16[256,2048]{1,0:T(8,128)(2,1)S(1)} collective-permute-done((bf16[256,2048]{1,0:T(8,128)(2,1)S(1)}, bf16[256,2048]{1,0:T(8,128)(2,1)S(1)}, u32[]{:S(2)}, u32[]{:S(2)}) %collective-permute-start.1) | collective-permute-done | bytes 1048608 | tf_op jit(solution)/shard_map/ppermute | solution.py:24
  192.3 12.3 %fusion.54 = f32[1024,1536]{1,0:T(8,128)} fusion(bf16[2048,1536]{1,0:T(8,128)(2,1)} %all-gather.3.cloned.1.call-done, bf16[1024,2048]{1,0:T(8,128)(2,1)} %copy-done, f32[2048]{0:T(1024)S(1)} %reshape.351, f32[2048]{0:T(1024)S(1)} %reshape.350, f32[1024]{0:T(1024)S(1)} %add_rsqrt_fusion, f32[1024]{0:T(1024)S(1)} %broadcast_multiply_fusion), kind=kOutput, calls=%fused_computation.157 | convolution fusion | flops 6455033856 | bytes 16801792 | tf_op jit(solution)/shard_map/dot_general | solution.py:205
  204.6 8.3 %reshape.331 = f32[1024,3,2,256]{3,2,1,0:T(2,128)} reshape(f32[1024,1536]{1,0:T(8,128)} %fusion.54) | data formatting | bytes 12582912 | tf_op jit(solution)/shard_map/reshape | solution.py:206
  218.1 3.8 fusion.55
  226.6 10.1 %fusion.61 = (f32[2,1024]{1,0:T(2,128)S(1)}, f32[2,1024,1024]{1,2,0:T(8,128)}) fusion(pred[1024,1024]{0,1:T(8,128)(4,1)} %compare_and_fusion, bf16[1024,2,192]{2,0,1:T(8,128)(2,1)S(1)} %slice.303, bf16[1024,2,64]{2,0,1:T(8,128)(2,1)} %get-tuple-element.158, bf16[1024,2,192]{2,0,1:T(8,128)(2,1)} %slice.304, bf16[1024,2,64]{2,0,1:T(8,128)(2,1)} %get-tuple-element.157), kind=kOutput, calls=%fused_computation.164 | convolution fusion | flops 1088422912 | bytes 11542528 | tf_op jit(solution)/shard_map/sub | solution.py:215
  236.8 4.7 fusion.25
  265.7 12.1 %convolution_convert_fusion.2 = bf16[2048,1536]{1,0:T(8,128)(2,1)S(1)} fusion(bf16[1024,1536]{0,1:T(8,128)(2,1)} %bitcast.197, bf16[1024,2048]{1,0:T(8,128)(2,1)} %copy-done, f32[2048]{0:T(1024)S(1)} %reshape.351, f32[2048]{0:T(1024)S(1)} %reshape.350, f32[1024]{0:T(1024)S(1)} %add_rsqrt_fusion, f32[1024]{0:T(1024)S(1)} %broadcast_multiply_fusion), kind=kOutput, calls=%fused_computation.37 | convolution fusion | flops 6458179584 | bytes 13656064 | tf_op jit(solution)/shard_map/dot_general | solution.py:103
  299.2 18.5 %fusion.7 = (f32[1024,2048]{1,0:T(8,128)S(1)}, bf16[1024,2048]{1,0:T(8,128)(2,1)}) fusion(bf16[2048,4096]{1,0:T(8,128)(2,1)} %all-gather.5.cloned.1.call-done, bf16[1024,2048]{1,0:T(8,128)(2,1)} %copy-done, f32[2048]{0:T(1024)S(1)} %reshape.355, f32[2048]{0:T(1024)S(1)} %reshape.354, f32[1024]{0:T(1024)S(1)} %add_rsqrt_fusion, ...), kind=kOutput, calls=%fused_computation.10 | convolution fusion | flops 8623489024 | bytes 25190400 | tf_op jit(solution)/shard_map/dot_general | solution.py:252
  317.7 12.2 %multiply_convert_fusion = bf16[1024,2048]{1,0:T(8,128)(2,1)S(1)} fusion(f32[1024,2048]{1,0:T(8,128)S(1)} %get-tuple-element.53, bf16[1024,2048]{0,1:T(8,128)(2,1)S(1)} %copy-done.31, bf16[2048,4096]{1,0:T(8,128)(2,1)} %all-gather.5.cloned.1.call-done), kind=kOutput, calls=%fused_computation.25 | convolution fusion | flops 8594128896 | bytes 25165824 | tf_op jit(solution)/shard_map/dot_general | solution.py:261
  329.9 10.9 %convolution_convert_fusion.1 = bf16[2048,2048]{1,0:T(8,128)(2,1)S(1)} fusion(bf16[1024,2048]{1,0:T(8,128)(2,1)S(1)} %multiply_convert_fusion, bf16[1024,2048]{1,0:T(8,128)(2,1)S(1)} %copy-done.1, f32[2048]{0:T(1024)S(1)} %reshape.355, f32[2048]{0:T(1024)S(1)} %reshape.354, f32[1024]{0:T(1024)S(1)} %add_rsqrt_fusion, f32[1024]{0:T(1024)S(1)} %broadcast_multiply_fusion), kind=kOutput, calls=%fused_computation.36 | convolution fusion | flops 8606711808 | bytes 16801792 | tf_op jit(solution)/shard_map/dot_general | solution.py:103
  341.7 12.4 %convolution_convert_fusion = bf16[2048,2048]{1,0:T(8,128)(2,1)S(1)} fusion(bf16[1024,2048]{0,1:T(8,128)(2,1)} %copy-done.29, bf16[1024,2048]{1,0:T(8,128)(2,1)} %get-tuple-element.55), kind=kOutput, calls=%fused_computation.35 | convolution fusion | flops 8594128896 | bytes 16777216 | tf_op jit(solution)/shard_map/dot_general | solution.py:103
  359.1 4.1 fusion.11
  366.2 5.5 fusion.10
  374.0 4.8 all-to-all-start.2
  378.9 13.1 %fusion.14 = f32[1024,2048]{1,0:T(8,128)S(1)} fusion(bf16[1024,2048]{1,0:T(8,128)(2,1)} %get-tuple-element.55, bf16[2048,4096]{1,0:T(8,128)(2,1)} %all-gather.5.cloned.1.call-done), kind=kOutput, calls=%fused_computation.23 | convolution fusion | flops 8589934592 | bytes 20971520 | tf_op jit(solution)/shard_map/dot_general | solution.py:267
  392.1 4.5 add_convert_fusion.1
  396.6 9.0 %fusion.62 = f32[1024,2048]{1,0:T(8,128)S(1)} fusion(bf16[1024,1536]{0,1:T(8,128)(2,1)S(1)} %bitcast.198, bf16[2048,1536]{1,0:T(8,128)(2,1)} %all-gather.3.cloned.1.call-done), kind=kOutput, calls=%fused_computation.165 | convolution fusion | flops 6442450944 | bytes 17825792 | tf_op jit(solution)/shard_map/dot_general | solution.py:273
  405.6 17.0 %add_convert_fusion = (bf16[1024,2048]{1,0:T(8,128)(2,1)}, f32[1024,2048]{1,0:T(8,128)}) fusion(f32[1024,2048]{1,0:T(8,128)S(1)} %fusion.62, f32[2048]{0:T(1024)S(1)} %reshape.354, f32[2048]{0:T(1024)S(1)} %reshape.350, bf16[1024,2048]{1,0:T(8,128)(2,1)S(1)} %copy-done.40, bf16[2048,4096]{1,0:T(8,128)(2,1)} %all-gather.5.cloned.1.call-done), kind=kOutput, calls=%fused_computation.19 | convolution fusion | flops 8598323200 | bytes 33570816 | tf_op jit(solution)/shard_map/dot_general | solution.py:272
  422.7 4.4 all-to-all-done.2
  427.0 4.9 copy.205
  435.3 11.6 %multiply_reduce_fusion.1 = (f32[2048]{0:T(1024)S(1)}, f32[2048]{0:T(1024)S(1)}, f32[2048]{0:T(1024)S(1)}, f32[2048]{0:T(1024)S(1)}, f32[1024,2048]{1,0:T(8,128)}) fusion(f32[1024,2048]{1,0:T(8,128)} %copy-done.6, bf16[1024,2048]{1,0:T(8,128)(2,1)} %copy-done, f32[1024]{0:T(1024)S(1)} %add_rsqrt_fusion, f32[1024]{0:T(1024)S(1)} %broadcast_multiply_fusion, ...), kind=kLoop, calls=%fused_computation.18 | loop fusion | flops 18866176 | bytes 29401088 | tf_op jit(solution)/shard_map/reduce_sum | solution.py:282
  474.2 26.8 %all-to-all-done.3 = f32[32,1,256]{2,1,0:T(1,128)S(1)} async-done(((f32[32,1,256]{2,1,0:T(1,128)}), f32[32,1,256]{2,1,0:T(1,128)S(1)}, u32[]{:S(2)}, u32[]{:S(2)}) %all-to-all-start.3) | async-done | bytes 32800 | tf_op jit(solution)/shard_map/all_to_all | solution.py:295
  501.0 4.2 all-to-all-start.4
  511.3 41.5 %all-to-all-done.4 = bf16[4,64,1536]{2,1,0:T(8,128)(2,1)} async-done(((bf16[4,64,1536]{2,1,0:T(8,128)(2,1)}), bf16[4,64,1536]{2,1,0:T(8,128)(2,1)}, u32[]{:S(2)}, u32[]{:S(2)}) %all-to-all-start.4) | async-done | bytes 786464 | tf_op jit(solution)/shard_map/all_to_all | solution.py:131
  552.8 4.5 all-to-all-start.5
  (269 shorter events, 177.8 us)
Async XLA Ops:
  7.2 185.1 %all-gather.3.cloned.1.call-start = ((), (), s32[]{:S(2)}) async-start(), calls=%async_computation.9 | async-start | bytes 7077888 | tf_op jit(solution)/shard_map/all_gather | solution.py:88
  27.6 271.6 %all-gather.5.cloned.1.call-start = ((), (), s32[]{:S(2)}) async-start(), calls=%async_computation.10 | async-start | bytes 18874368 | tf_op jit(solution)/shard_map/all_gather | solution.py:88
  68.1 386.3 %reduce-scatter.4.cloned.1.call-start = ((), (), s32[]{:S(2)}) async-start(), calls=%async_computation.11 | async-start | bytes 5242880 | tf_op jit(solution)/shard_map/reduce_scatter | solution.py:113
  68.2 25.4 %collective-permute-start.3 = (bf16[64,2048]{1,0:T(8,128)(2,1)S(1)}, bf16[64,2048]{1,0:T(8,128)(2,1)S(1)}, u32[]{:S(2)}, u32[]{:S(2)}) collective-permute-start(bf16[64,2048]{1,0:T(8,128)(2,1)S(1)} %copy-done.22), channel_id=1, source_target_pairs={{0,2},{2,0},{4,6},{6,4},{1,3},{3,1},{5,7},{7,5},{8,10},{10,8},{12,... | collective-permute-start | bytes 786440 | tf_op jit(solution)/shard_map/ppermute | solution.py:93
  69.8 26.5 %collective-permute-start.5 = (bf16[64,2048]{1,0:T(8,128)(2,1)S(1)}, bf16[64,2048]{1,0:T(8,128)(2,1)S(1)}, u32[]{:S(2)}, u32[]{:S(2)}) collective-permute-start(bf16[64,2048]{1,0:T(8,128)(2,1)S(1)} %copy-done.22), channel_id=1, source_target_pairs={{0,6},{2,4},{4,2},{6,0},{1,7},{3,5},{5,3},{7,1},{8,14},{10,12},{12... | collective-permute-start | bytes 786440 | tf_op jit(solution)/shard_map/ppermute | solution.py:93
  72.3 40.6 %collective-permute-start.4 = (bf16[64,2048]{1,0:T(8,128)(2,1)S(1)}, bf16[64,2048]{1,0:T(8,128)(2,1)S(1)}, u32[]{:S(2)}, u32[]{:S(2)}) collective-permute-start(bf16[64,2048]{1,0:T(8,128)(2,1)S(1)} %copy-done.22), channel_id=1, source_target_pairs={{0,4},{2,6},{4,0},{6,2},{1,5},{3,7},{5,1},{7,3},{8,12},{10,14},{12... | collective-permute-start | bytes 786440 | tf_op jit(solution)/shard_map/ppermute | solution.py:93
  114.0 3.2 collective-permute-start.6
  133.8 7.1 %collective-permute-start.7 = (s32[1,2,256]{2,1,0:T(2,128)S(1)}, s32[1,2,256]{2,1,0:T(2,128)S(1)}, u32[]{:S(2)}, u32[]{:S(2)}) collective-permute-start(s32[1,2,256]{2,1,0:T(2,128)S(1)} %add_bitcast_fusion), channel_id=1, source_target_pairs={{0,8},{8,0},{16,24},{24,16},{1,9},{9,1},{17,25},{25,17},{2,10},{10... | collective-permute-start | bytes 6152 | tf_op jit(solution)/shard_map/ppermute | solution.py:24
  135.2 6.3 %collective-permute-start.9 = (s32[1,2,256]{2,1,0:T(2,128)S(1)}, s32[1,2,256]{2,1,0:T(2,128)S(1)}, u32[]{:S(2)}, u32[]{:S(2)}) collective-permute-start(s32[1,2,256]{2,1,0:T(2,128)S(1)} %add_bitcast_fusion), channel_id=1, source_target_pairs={{0,24},{8,16},{16,8},{24,0},{1,25},{9,17},{17,9},{25,1},{2,26},{10... | collective-permute-start | bytes 6152 | tf_op jit(solution)/shard_map/ppermute | solution.py:24
  136.7 4.8 collective-permute-start.8
  137.9 27.0 %collective-permute-start.2 = (bf16[256,2048]{1,0:T(8,128)(2,1)S(1)}, bf16[256,2048]{1,0:T(8,128)(2,1)S(1)}, u32[]{:S(2)}, u32[]{:S(2)}) collective-permute-start(bf16[256,2048]{1,0:T(8,128)(2,1)S(1)} %copy.177), channel_id=1, source_target_pairs={{0,24},{8,16},{16,8},{24,0},{1,25},{9,17},{17,9},{25,1},{2,26},{10... | collective-permute-start | bytes 3145736 | tf_op jit(solution)/shard_map/ppermute | solution.py:24
  140.3 45.8 %collective-permute-start.1 = (bf16[256,2048]{1,0:T(8,128)(2,1)S(1)}, bf16[256,2048]{1,0:T(8,128)(2,1)S(1)}, u32[]{:S(2)}, u32[]{:S(2)}) collective-permute-start(bf16[256,2048]{1,0:T(8,128)(2,1)S(1)} %copy.177), channel_id=1, source_target_pairs={{0,16},{8,24},{16,0},{24,8},{1,17},{9,25},{17,1},{25,9},{2,18},{10... | collective-permute-start | bytes 3145736 | tf_op jit(solution)/shard_map/ppermute | solution.py:24
  140.9 45.3 %collective-permute-start = (bf16[256,2048]{1,0:T(8,128)(2,1)S(1)}, bf16[256,2048]{1,0:T(8,128)(2,1)S(1)}, u32[]{:S(2)}, u32[]{:S(2)}) collective-permute-start(bf16[256,2048]{1,0:T(8,128)(2,1)S(1)} %copy.177), channel_id=1, source_target_pairs={{0,8},{8,0},{16,24},{24,16},{1,9},{9,1},{17,25},{25,17},{2,10},{10... | collective-permute-start | bytes 3145736 | tf_op jit(solution)/shard_map/ppermute | solution.py:24
  186.8 56.9 %collective-permute-start.12 = (bf16[256,2048]{0,1:T(8,128)(2,1)S(1)}, bf16[256,2048]{0,1:T(8,128)(2,1)}, u32[]{:S(2)}, u32[]{:S(2)}) collective-permute-start(bf16[256,2048]{0,1:T(8,128)(2,1)S(1)} %bitcast.171), channel_id=1, source_target_pairs={{0,24},{8,16},{16,8},{24,0},{1,25},{9,17},{17,9},{25,1},{2,26},{10... | collective-permute-start | bytes 3145736 | tf_op jit(solution)/shard_map/ppermute | solution.py:24
  188.6 55.2 %collective-permute-start.11 = (bf16[256,2048]{0,1:T(8,128)(2,1)S(1)}, bf16[256,2048]{0,1:T(8,128)(2,1)}, u32[]{:S(2)}, u32[]{:S(2)}) collective-permute-start(bf16[256,2048]{0,1:T(8,128)(2,1)S(1)} %bitcast.172), channel_id=1, source_target_pairs={{0,16},{8,24},{16,0},{24,8},{1,17},{9,25},{17,1},{25,9},{2,18},{10... | collective-permute-start | bytes 3145736 | tf_op jit(solution)/shard_map/ppermute | solution.py:24
  189.8 54.0 %collective-permute-start.10 = (bf16[256,2048]{0,1:T(8,128)(2,1)S(1)}, bf16[256,2048]{0,1:T(8,128)(2,1)}, u32[]{:S(2)}, u32[]{:S(2)}) collective-permute-start(bf16[256,2048]{0,1:T(8,128)(2,1)S(1)} %bitcast.173), channel_id=1, source_target_pairs={{0,8},{8,0},{16,24},{24,16},{1,9},{9,1},{17,25},{25,17},{2,10},{10... | collective-permute-start | bytes 3145736 | tf_op jit(solution)/shard_map/ppermute | solution.py:24
  278.0 14.3 %collective-permute-start.13 = (bf16[4,256,1536]{2,1,0:T(8,128)(2,1)S(1)}, bf16[4,256,1536]{2,1,0:T(8,128)(2,1)}, u32[]{:S(2)}, u32[]{:S(2)}) collective-permute-start(bf16[4,256,1536]{2,1,0:T(8,128)(2,1)S(1)} %dynamic-slice_bitcast_fusion.2), channel_id=1, source_target_pairs={{0,1},{1,0},{2,3},{3,2},{4,5},{5,4},{6,7},{7,6},{8,9},{9,8},{10,11... | collective-permute-start | bytes 9437192 | tf_op jit(solution)/shard_map/ppermute | solution.py:106
  287.3 3.0 collective-permute-start.14
  298.7 212.5 %reduce-scatter.6.cloned.1.call-start = ((), (), s32[]{:S(2)}) async-start(), calls=%async_computation.12 | async-start | bytes 5242880 | tf_op jit(solution)/shard_map/reduce_scatter | solution.py:113
  341.5 17.6 %collective-permute-start.15 = (bf16[4,256,2048]{2,1,0:T(8,128)(2,1)S(1)}, bf16[4,256,2048]{2,1,0:T(8,128)(2,1)S(1)}, u32[]{:S(2)}, u32[]{:S(2)}) collective-permute-start(bf16[4,256,2048]{2,1,0:T(8,128)(2,1)S(1)} %dynamic-slice_bitcast_fusion.1), channel_id=1, source_target_pairs={{0,1},{1,0},{2,3},{3,2},{4,5},{5,4},{6,7},{7,6},{8,9},{9,8},{10,11... | collective-permute-start | bytes 12582920 | tf_op jit(solution)/shard_map/ppermute | solution.py:106
  358.7 7.5 %collective-permute-start.19 = (bf16[4,256,2048]{2,1,0:T(8,128)(2,1)}, bf16[4,256,2048]{2,1,0:T(8,128)(2,1)}, u32[]{:S(2)}, u32[]{:S(2)}) collective-permute-start(bf16[4,256,2048]{2,1,0:T(8,128)(2,1)} %dynamic-slice_bitcast_fusion), channel_id=1, source_target_pairs={{0,1},{1,0},{2,3},{3,2},{4,5},{5,4},{6,7},{7,6},{8,9},{9,8},{10,11... | collective-permute-start | bytes 12582920 | tf_op jit(solution)/shard_map/ppermute | solution.py:106
  374.0 53.0 %all-to-all-start.2 = ((bf16[4,4,64,2048]{3,2,1,0:T(8,128)(2,1)}), bf16[4,4,64,2048]{3,2,1,0:T(8,128)(2,1)}, u32[]{:S(2)}, u32[]{:S(2)}) async-start(bf16[4,4,64,2048]{3,2,1,0:T(8,128)(2,1)} %copy.204), calls=%async_computation.2 | async-start | bytes 8388608 | tf_op jit(solution)/shard_map/all_to_all | solution.py:138
  378.9 200.0 %reduce-scatter.8.cloned.1.call-start = ((), (), s32[]{:S(2)}) async-start(), calls=%async_computation.13 | async-start | bytes 5242880 | tf_op jit(solution)/shard_map/reduce_scatter | solution.py:113
  450.9 54.9 %collective-permute-start.22 = (bf16[256,2048]{1,0:T(8,128)(2,1)}, bf16[256,2048]{1,0:T(8,128)(2,1)S(1)}, u32[]{:S(2)}, u32[]{:S(2)}) collective-permute-start(bf16[256,2048]{1,0:T(8,128)(2,1)} %get-tuple-element.127), channel_id=1, source_target_pairs={{0,24},{8,16},{16,8},{24,0},{1,25},{9,17},{17,9},{25,1},{2,26},{10... | collective-permute-start | bytes 3145736 | tf_op jit(solution)/shard_map/ppermute | solution.py:24
  452.2 55.6 %collective-permute-start.21 = (bf16[256,2048]{1,0:T(8,128)(2,1)}, bf16[256,2048]{1,0:T(8,128)(2,1)S(1)}, u32[]{:S(2)}, u32[]{:S(2)}) collective-permute-start(bf16[256,2048]{1,0:T(8,128)(2,1)} %get-tuple-element.128), channel_id=1, source_target_pairs={{0,16},{8,24},{16,0},{24,8},{1,17},{9,25},{17,1},{25,9},{2,18},{10... | collective-permute-start | bytes 3145736 | tf_op jit(solution)/shard_map/ppermute | solution.py:24
  453.7 54.1 %collective-permute-start.20 = (bf16[256,2048]{1,0:T(8,128)(2,1)}, bf16[256,2048]{1,0:T(8,128)(2,1)}, u32[]{:S(2)}, u32[]{:S(2)}) collective-permute-start(bf16[256,2048]{1,0:T(8,128)(2,1)} %get-tuple-element.129), channel_id=1, source_target_pairs={{0,8},{8,0},{16,24},{24,16},{1,9},{9,1},{17,25},{25,17},{2,10},{10... | collective-permute-start | bytes 3145736 | tf_op jit(solution)/shard_map/ppermute | solution.py:24
  455.2 45.8 %all-to-all-start.3 = ((f32[32,1,256]{2,1,0:T(1,128)}), f32[32,1,256]{2,1,0:T(1,128)S(1)}, u32[]{:S(2)}, u32[]{:S(2)}) async-start(f32[32,1,256]{2,1,0:T(1,128)} %all_to_all.28), calls=%async_computation.3 | async-start | bytes 65536 | tf_op jit(solution)/shard_map/all_to_all | solution.py:295
  471.1 100.0 %collective-permute-start.18 = (bf16[256,2048]{1,0:T(8,128)(2,1)}, bf16[256,2048]{1,0:T(8,128)(2,1)}, u32[]{:S(2)}, u32[]{:S(2)}) collective-permute-start(bf16[256,2048]{1,0:T(8,128)(2,1)} %get-tuple-element.130), channel_id=1, source_target_pairs={{0,24},{8,16},{16,8},{24,0},{1,25},{9,17},{17,9},{25,1},{2,26},{10... | collective-permute-start | bytes 3145736 | tf_op jit(solution)/shard_map/ppermute | solution.py:24
  473.6 97.4 %collective-permute-start.17 = (bf16[256,2048]{1,0:T(8,128)(2,1)}, bf16[256,2048]{1,0:T(8,128)(2,1)}, u32[]{:S(2)}, u32[]{:S(2)}) collective-permute-start(bf16[256,2048]{1,0:T(8,128)(2,1)} %get-tuple-element.131), channel_id=1, source_target_pairs={{0,16},{8,24},{16,0},{24,8},{1,17},{9,25},{17,1},{25,9},{2,18},{10... | collective-permute-start | bytes 3145736 | tf_op jit(solution)/shard_map/ppermute | solution.py:24
  501.0 51.8 %all-to-all-start.4 = ((bf16[4,64,1536]{2,1,0:T(8,128)(2,1)}), bf16[4,64,1536]{2,1,0:T(8,128)(2,1)}, u32[]{:S(2)}, u32[]{:S(2)}) async-start(bf16[4,64,1536]{2,1,0:T(8,128)(2,1)} %bitcast.200), calls=%async_computation.5 | async-start | bytes 1572864 | tf_op jit(solution)/shard_map/all_to_all | solution.py:131
  505.8 65.2 %collective-permute-start.16 = (bf16[256,2048]{1,0:T(8,128)(2,1)}, bf16[256,2048]{1,0:T(8,128)(2,1)}, u32[]{:S(2)}, u32[]{:S(2)}) collective-permute-start(bf16[256,2048]{1,0:T(8,128)(2,1)} %get-tuple-element.132), channel_id=1, source_target_pairs={{0,8},{8,0},{16,24},{24,16},{1,9},{9,1},{17,25},{25,17},{2,10},{10... | collective-permute-start | bytes 3145736 | tf_op jit(solution)/shard_map/ppermute | solution.py:24
  552.8 23.4 %all-to-all-start.5 = ((bf16[4,64,2048]{2,1,0:T(8,128)(2,1)}), bf16[4,64,2048]{2,1,0:T(8,128)(2,1)}, u32[]{:S(2)}, u32[]{:S(2)}) async-start(bf16[4,64,2048]{2,1,0:T(8,128)(2,1)} %bitcast.206), calls=%async_computation.7 | async-start | bytes 2097152 | tf_op jit(solution)/shard_map/all_to_all | solution.py:131
  (45 other events, 993.2 us)
Sparse Core Ops, SparseCore 0:
  27.7 85.0 all-gather.2
  114.4 150.0 all-gather.4
  298.8 74.5 reduce-scatter.3
  375.6 77.2 reduce-scatter.5
  455.1 77.2 reduce-scatter.7

commit v4 on v3

--- a/solution.py
+++ b/solution.py
@@ -273,7 +273,8 @@
     grad_first = lax.dot_general(grad_projected, qkv, COLS_BOTH, preferred_element_type=f32)
     scaled = (grad_first * gain_one + grad_second * gain_two).astype(bf16)
     grad_first, grad_second, scaled = lax.optimization_barrier((grad_first, grad_second, scaled))
-    ready_down = after(ready_down, scaled).swapaxes(0, 1).reshape(pair_down.shape)
+    ready_down = after(ready_down, scaled).transpose(1, 2, 0, 3)
+    ready_down = ready_down.reshape(-1, ctx_count * pair_down.shape[1])
     summed_down = sum_rows(ready_down)
     output = scatter_ctx(branches, rows, ready_down) + own_tokens.astype(f32)
     output = outer(output.astype(bf16))[None]
@@ -300,6 +301,7 @@
     second_mean = jnp.mean(scaled * own_normed, axis=-1, keepdims=True)
     back = (scaled - first_mean - own_normed * second_mean) * inv_std[:rows]
     grad_tokens = outer((own_grads.astype(f32) + back).astype(bf16))[None]
+    grad_up = return_columns(summed_up, 1, grad_tokens)
     return (
         output,
         grad_tokens,
@@ -309,8 +311,8 @@
         norm_sums[3],
         return_columns(summed_qkv, 3, grad_tokens),
         outer(summed_out.astype(f32)),
-        return_columns(summed_up, 1, grad_tokens),
-        row_shard(summed_down.reshape(ctx_count, -1, summed_down.shape[1]), 1),
+        grad_up,
+        summed_down.astype(f32),
     )
 
 

time: 595 us -> 602 us (1.012)
    unnamed x97 -> x98, local copies, waits for them, and re-layouts: 21.7 us -> 28.2 us
  transfers between devices with their start and end apart: 32 -> 32, of which waited for: 10 -> 10; matrix products, arithmetic and copies ran while one was open for 53% -> 54% of each run, Pallas kernels for 0% -> 0%
where the time goes in v4:
time: 602 us; the launch traced here: 596 us
  waiting for transfers between devices  159 us (26%)
  matrix products  146 us (24%)
  local copies, waits for them, and re-layouts  124 us (21%)
  other arithmetic  67.2 us (11%)
  blocking collectives  44.1 us (7%)
  starting transfers between devices  40.7 us (7%)
  between operations  15.2 us (3%)
    all_to_all x2, blocking collectives, exchange_columns(): mine = lax.all_to_all(split, 'ctx', 0, 0, tiled=True)  44.1 us
    all_to_all x2, waiting for transfers between devices, return_columns(): mine = lax.all_to_all(split, 'ctx', 0, 0, tiled=True)  41.5 us
    ppermute x3, waiting for transfers between devices, gather_small(): lax.ppermute(mine, 'line', [(i, i ^ k) for i in range(lines)])  40.4 us
    ppermute x15, waiting for transfers between devices, swap(): return lax.ppermute(value, 'ctx', [(i, i ^ step) for i in range(count)])  39.7 us
    dot_general x4, matrix products, sum_pair(): lax.dot_general(left, right, ROWS_FIRST, preferred_element_type=jnp.float32)  37.8 us
    unnamed x98, local copies, waits for them, and re-layouts  28.2 us
    all_to_all x1, waiting for transfers between devices, on_device(): norm_sums = lax.all_to_all(norm_terms, ('ctx', *FSDP), 0, 0, tiled=True)  26.8 us
    ppermute x15, starting transfers between devices, swap(): return lax.ppermute(value, 'ctx', [(i, i ^ step) for i in range(count)])  19.2 us
  transfers between devices with their start and end apart: 32, of which 10 were waited for; matrix products, arithmetic and copies ran while one was open for 54% of the time, Pallas kernels for 0%

profile of v4, /device:TPU:0, one launch (start us, length us, event | category | flops | bytes accessed | tf_op | source)
XLA Modules:
  0.0 595.5 jit_solution(13365381507045651353)
XLA Ops:
  11.2 16.4 %all_to_all.35 = bf16[4,64,1536]{2,1,0:T(8,128)(2,1)} all-to-all(bf16[4,64,1536]{2,1,0:T(8,128)(2,1)S(1)} %reshape.316), channel_id=1, replica_groups=mesh['ctx'=4,'line'=4,'core'=2] {'ctx'}, dimensions={0} | all-to-all | bytes 1572864 | tf_op jit(solution)/shard_map/all_to_all | solution.py:83
  40.5 27.6 %all_to_all.36 = bf16[4,64,4096]{2,1,0:T(8,128)(2,1)} all-to-all(bf16[4,64,4096]{2,1,0:T(8,128)(2,1)S(1)} %reshape.314), channel_id=1, replica_groups=mesh['ctx'=4,'line'=4,'core'=2] {'ctx'}, dimensions={0} | all-to-all | bytes 4194304 | tf_op jit(solution)/shard_map/all_to_all | solution.py:83
  72.4 21.1 %collective-permute-done.3 = bf16[64,2048]{1,0:T(8,128)(2,1)S(1)} collective-permute-done((bf16[64,2048]{1,0:T(8,128)(2,1)S(1)}, bf16[64,2048]{1,0:T(8,128)(2,1)S(1)}, u32[]{:S(2)}, u32[]{:S(2)}) %collective-permute-start.3) | collective-permute-done | bytes 262176 | tf_op jit(solution)/shard_map/ppermute | solution.py:93
  96.3 16.6 %collective-permute-done.4 = bf16[64,2048]{1,0:T(8,128)(2,1)S(1)} collective-permute-done((bf16[64,2048]{1,0:T(8,128)(2,1)S(1)}, bf16[64,2048]{1,0:T(8,128)(2,1)S(1)}, u32[]{:S(2)}, u32[]{:S(2)}) %collective-permute-start.4) | collective-permute-done | bytes 262176 | tf_op jit(solution)/shard_map/ppermute | solution.py:93
  121.1 7.2 %reshape_reshape.9 = bf16[512,4,8,64]{3,2,1,0:T(8,128)(2,1)} reshape(bf16[4,2,64,2048]{3,2,1,0:T(8,128)(2,1)} %copy.181) | data formatting | bytes 4194304 | tf_op jit(solution)/shard_map/reshape;reshape | solution.py:44
  128.3 5.4 copy.182
  146.5 18.5 %collective-permute-done.2 = bf16[256,2048]{1,0:T(8,128)(2,1)S(1)} collective-permute-done((bf16[256,2048]{1,0:T(8,128)(2,1)S(1)}, bf16[256,2048]{1,0:T(8,128)(2,1)S(1)}, u32[]{:S(2)}, u32[]{:S(2)}) %collective-permute-start.2) | collective-permute-done | bytes 1048608 | tf_op jit(solution)/shard_map/ppermute | solution.py:24
  164.9 21.2 %collective-permute-done.1 = bf16[256,2048]{1,0:T(8,128)(2,1)S(1)} collective-permute-done((bf16[256,2048]{1,0:T(8,128)(2,1)S(1)}, bf16[256,2048]{1,0:T(8,128)(2,1)S(1)}, u32[]{:S(2)}, u32[]{:S(2)}) %collective-permute-start.1) | collective-permute-done | bytes 1048608 | tf_op jit(solution)/shard_map/ppermute | solution.py:24
  192.3 12.3 %fusion.54 = f32[1024,1536]{1,0:T(8,128)} fusion(bf16[2048,1536]{1,0:T(8,128)(2,1)} %all-gather.3.cloned.1.call-done, bf16[1024,2048]{1,0:T(8,128)(2,1)} %copy-done, f32[2048]{0:T(1024)S(1)} %reshape.342, f32[2048]{0:T(1024)S(1)} %reshape.341, f32[1024]{0:T(1024)S(1)} %add_rsqrt_fusion, f32[1024]{0:T(1024)S(1)} %broadcast_multiply_fusion), kind=kOutput, calls=%fused_computation.156 | convolution fusion | flops 6455033856 | bytes 16801792 | tf_op jit(solution)/shard_map/dot_general | solution.py:205
  204.5 8.3 %reshape.322 = f32[1024,3,2,256]{3,2,1,0:T(2,128)} reshape(f32[1024,1536]{1,0:T(8,128)} %fusion.54) | data formatting | bytes 12582912 | tf_op jit(solution)/shard_map/reshape | solution.py:206
  226.6 10.1 %fusion.60 = (f32[2,1024]{1,0:T(2,128)S(1)}, f32[2,1024,1024]{1,2,0:T(8,128)}) fusion(pred[1024,1024]{0,1:T(8,128)(4,1)} %compare_and_fusion, bf16[1024,2,192]{2,0,1:T(8,128)(2,1)S(1)} %slice.279, bf16[1024,2,64]{2,0,1:T(8,128)(2,1)} %get-tuple-element.154, bf16[1024,2,192]{2,0,1:T(8,128)(2,1)} %slice.280, bf16[1024,2,64]{2,0,1:T(8,128)(2,1)} %get-tuple-element.153), kind=kOutput, calls=%fused_computation.162 | convolution fusion | flops 1088422912 | bytes 11542528 | tf_op jit(solution)/shard_map/sub | solution.py:215
  236.7 4.7 fusion.25
  265.7 12.1 %convolution_convert_fusion.2 = bf16[2048,1536]{1,0:T(8,128)(2,1)S(1)} fusion(bf16[1024,1536]{0,1:T(8,128)(2,1)} %bitcast.199, bf16[1024,2048]{1,0:T(8,128)(2,1)} %copy-done, f32[2048]{0:T(1024)S(1)} %reshape.342, f32[2048]{0:T(1024)S(1)} %reshape.341, f32[1024]{0:T(1024)S(1)} %add_rsqrt_fusion, f32[1024]{0:T(1024)S(1)} %broadcast_multiply_fusion), kind=kOutput, calls=%fused_computation.37 | convolution fusion | flops 6458179584 | bytes 13656064 | tf_op jit(solution)/shard_map/dot_general | solution.py:103
  299.2 18.5 %fusion.7 = (f32[1024,2048]{1,0:T(8,128)S(1)}, bf16[1024,2048]{1,0:T(8,128)(2,1)}) fusion(bf16[2048,4096]{1,0:T(8,128)(2,1)} %all-gather.5.cloned.1.call-done, bf16[1024,2048]{1,0:T(8,128)(2,1)} %copy-done, f32[2048]{0:T(1024)S(1)} %reshape.346, f32[2048]{0:T(1024)S(1)} %reshape.345, f32[1024]{0:T(1024)S(1)} %add_rsqrt_fusion, ...), kind=kOutput, calls=%fused_computation.10 | convolution fusion | flops 8623489024 | bytes 25190400 | tf_op jit(solution)/shard_map/dot_general | solution.py:252
  317.6 12.2 %multiply_convert_fusion = bf16[1024,2048]{1,0:T(8,128)(2,1)S(1)} fusion(f32[1024,2048]{1,0:T(8,128)S(1)} %get-tuple-element.53, bf16[1024,2048]{0,1:T(8,128)(2,1)S(1)} %copy-done.31, bf16[2048,4096]{1,0:T(8,128)(2,1)} %all-gather.5.cloned.1.call-done), kind=kOutput, calls=%fused_computation.25 | convolution fusion | flops 8594128896 | bytes 25165824 | tf_op jit(solution)/shard_map/dot_general | solution.py:261
  329.9 10.9 %convolution_convert_fusion.1 = bf16[2048,2048]{1,0:T(8,128)(2,1)S(1)} fusion(bf16[1024,2048]{1,0:T(8,128)(2,1)S(1)} %multiply_convert_fusion, bf16[1024,2048]{1,0:T(8,128)(2,1)S(1)} %copy-done.1, f32[2048]{0:T(1024)S(1)} %reshape.346, f32[2048]{0:T(1024)S(1)} %reshape.345, f32[1024]{0:T(1024)S(1)} %add_rsqrt_fusion, f32[1024]{0:T(1024)S(1)} %broadcast_multiply_fusion), kind=kOutput, calls=%fused_computation.36 | convolution fusion | flops 8606711808 | bytes 16801792 | tf_op jit(solution)/shard_map/dot_general | solution.py:103
  341.6 12.4 %convolution_convert_fusion = bf16[2048,2048]{1,0:T(8,128)(2,1)S(1)} fusion(bf16[1024,2048]{0,1:T(8,128)(2,1)} %copy-done.29, bf16[1024,2048]{1,0:T(8,128)(2,1)} %get-tuple-element.55), kind=kOutput, calls=%fused_computation.35 | convolution fusion | flops 8594128896 | bytes 16777216 | tf_op jit(solution)/shard_map/dot_general | solution.py:103
  359.0 4.1 fusion.11
  366.1 5.5 fusion.10
  374.0 4.8 all-to-all-start.2
  378.9 13.1 %fusion.14 = f32[1024,2048]{1,0:T(8,128)S(1)} fusion(bf16[1024,2048]{1,0:T(8,128)(2,1)} %get-tuple-element.55, bf16[2048,4096]{1,0:T(8,128)(2,1)} %all-gather.5.cloned.1.call-done), kind=kOutput, calls=%fused_computation.23 | convolution fusion | flops 8589934592 | bytes 20971520 | tf_op jit(solution)/shard_map/dot_general | solution.py:267
  392.0 4.5 add_convert_fusion.1
  396.5 9.1 %fusion.61 = f32[1024,2048]{1,0:T(8,128)S(1)} fusion(bf16[1024,1536]{0,1:T(8,128)(2,1)S(1)} %bitcast.200, bf16[2048,1536]{1,0:T(8,128)(2,1)} %all-gather.3.cloned.1.call-done), kind=kOutput, calls=%fused_computation.163 | convolution fusion | flops 6442450944 | bytes 17825792 | tf_op jit(solution)/shard_map/dot_general | solution.py:273
  405.5 17.0 %add_convert_fusion = (bf16[1024,2048]{1,0:T(8,128)(2,1)}, f32[1024,2048]{1,0:T(8,128)}) fusion(f32[1024,2048]{1,0:T(8,128)S(1)} %fusion.61, f32[2048]{0:T(1024)S(1)} %reshape.345, f32[2048]{0:T(1024)S(1)} %reshape.341, bf16[1024,2048]{1,0:T(8,128)(2,1)S(1)} %copy-done.40, bf16[2048,4096]{1,0:T(8,128)(2,1)} %all-gather.5.cloned.1.call-done), kind=kOutput, calls=%fused_computation.19 | convolution fusion | flops 8598323200 | bytes 33570816 | tf_op jit(solution)/shard_map/dot_general | solution.py:272
  422.6 4.4 all-to-all-done.2
  427.0 5.6 copy.208
  432.5 6.4 %copy.239 = bf16[32,8,4,2048]{3,1,2,0:T(8,128)(2,1)} copy(bf16[32,8,4,2048]{3,2,1,0:T(4,128)(2,1)S(1)} %bitcast.169) | data formatting | bytes 8388608
  442.5 11.6 %multiply_reduce_fusion.1 = (f32[2048]{0:T(1024)S(1)}, f32[2048]{0:T(1024)S(1)}, f32[2048]{0:T(1024)S(1)}, f32[2048]{0:T(1024)S(1)}, f32[1024,2048]{1,0:T(8,128)}) fusion(f32[1024,2048]{1,0:T(8,128)} %copy-done.6, bf16[1024,2048]{1,0:T(8,128)(2,1)} %copy-done, f32[1024]{0:T(1024)S(1)} %add_rsqrt_fusion, f32[1024]{0:T(1024)S(1)} %broadcast_multiply_fusion, ...), kind=kLoop, calls=%fused_computation.18 | loop fusion | flops 18866176 | bytes 29401088 | tf_op jit(solution)/shard_map/reduce_sum | solution.py:283
  481.3 26.8 %all-to-all-done.3 = f32[32,1,256]{2,1,0:T(1,128)S(1)} async-done(((f32[32,1,256]{2,1,0:T(1,128)}), f32[32,1,256]{2,1,0:T(1,128)S(1)}, u32[]{:S(2)}, u32[]{:S(2)}) %all-to-all-start.3) | async-done | bytes 32800 | tf_op jit(solution)/shard_map/all_to_all | solution.py:296
  508.1 4.2 all-to-all-start.4
  518.5 41.5 %all-to-all-done.4 = bf16[4,64,1536]{2,1,0:T(8,128)(2,1)} async-done(((bf16[4,64,1536]{2,1,0:T(8,128)(2,1)}), bf16[4,64,1536]{2,1,0:T(8,128)(2,1)}, u32[]{:S(2)}, u32[]{:S(2)}) %all-to-all-start.4) | async-done | bytes 786464 | tf_op jit(solution)/shard_map/all_to_all | solution.py:131
  559.9 4.5 all-to-all-start.5
  (269 shorter events, 181.8 us)
Async XLA Ops:
  7.2 185.1 %all-gather.3.cloned.1.call-start = ((), (), s32[]{:S(2)}) async-start(), calls=%async_computation.9 | async-start | bytes 7077888 | tf_op jit(solution)/shard_map/all_gather | solution.py:88
  27.6 271.5 %all-gather.5.cloned.1.call-start = ((), (), s32[]{:S(2)}) async-start(), calls=%async_computation.10 | async-start | bytes 18874368 | tf_op jit(solution)/shard_map/all_gather | solution.py:88
  68.1 393.4 %reduce-scatter.4.cloned.1.call-start = ((), (), s32[]{:S(2)}) async-start(), calls=%async_computation.11 | async-start | bytes 5242880 | tf_op jit(solution)/shard_map/reduce_scatter | solution.py:113
  68.2 25.4 %collective-permute-start.3 = (bf16[64,2048]{1,0:T(8,128)(2,1)S(1)}, bf16[64,2048]{1,0:T(8,128)(2,1)S(1)}, u32[]{:S(2)}, u32[]{:S(2)}) collective-permute-start(bf16[64,2048]{1,0:T(8,128)(2,1)S(1)} %copy-done.22), channel_id=1, source_target_pairs={{0,2},{2,0},{4,6},{6,4},{1,3},{3,1},{5,7},{7,5},{8,10},{10,8},{12,... | collective-permute-start | bytes 786440 | tf_op jit(solution)/shard_map/ppermute | solution.py:93
  69.8 26.5 %collective-permute-start.5 = (bf16[64,2048]{1,0:T(8,128)(2,1)S(1)}, bf16[64,2048]{1,0:T(8,128)(2,1)S(1)}, u32[]{:S(2)}, u32[]{:S(2)}) collective-permute-start(bf16[64,2048]{1,0:T(8,128)(2,1)S(1)} %copy-done.22), channel_id=1, source_target_pairs={{0,6},{2,4},{4,2},{6,0},{1,7},{3,5},{5,3},{7,1},{8,14},{10,12},{12... | collective-permute-start | bytes 786440 | tf_op jit(solution)/shard_map/ppermute | solution.py:93
  72.3 40.6 %collective-permute-start.4 = (bf16[64,2048]{1,0:T(8,128)(2,1)S(1)}, bf16[64,2048]{1,0:T(8,128)(2,1)S(1)}, u32[]{:S(2)}, u32[]{:S(2)}) collective-permute-start(bf16[64,2048]{1,0:T(8,128)(2,1)S(1)} %copy-done.22), channel_id=1, source_target_pairs={{0,4},{2,6},{4,0},{6,2},{1,5},{3,7},{5,1},{7,3},{8,12},{10,14},{12... | collective-permute-start | bytes 786440 | tf_op jit(solution)/shard_map/ppermute | solution.py:93
  114.0 3.2 collective-permute-start.6
  133.8 7.1 %collective-permute-start.7 = (s32[1,2,256]{2,1,0:T(2,128)S(1)}, s32[1,2,256]{2,1,0:T(2,128)S(1)}, u32[]{:S(2)}, u32[]{:S(2)}) collective-permute-start(s32[1,2,256]{2,1,0:T(2,128)S(1)} %add_bitcast_fusion), channel_id=1, source_target_pairs={{0,8},{8,0},{16,24},{24,16},{1,9},{9,1},{17,25},{25,17},{2,10},{10... | collective-permute-start | bytes 6152 | tf_op jit(solution)/shard_map/ppermute | solution.py:24
  135.2 6.3 %collective-permute-start.9 = (s32[1,2,256]{2,1,0:T(2,128)S(1)}, s32[1,2,256]{2,1,0:T(2,128)S(1)}, u32[]{:S(2)}, u32[]{:S(2)}) collective-permute-start(s32[1,2,256]{2,1,0:T(2,128)S(1)} %add_bitcast_fusion), channel_id=1, source_target_pairs={{0,24},{8,16},{16,8},{24,0},{1,25},{9,17},{17,9},{25,1},{2,26},{10... | collective-permute-start | bytes 6152 | tf_op jit(solution)/shard_map/ppermute | solution.py:24
  136.7 4.8 collective-permute-start.8
  137.9 27.0 %collective-permute-start.2 = (bf16[256,2048]{1,0:T(8,128)(2,1)S(1)}, bf16[256,2048]{1,0:T(8,128)(2,1)S(1)}, u32[]{:S(2)}, u32[]{:S(2)}) collective-permute-start(bf16[256,2048]{1,0:T(8,128)(2,1)S(1)} %copy.180), channel_id=1, source_target_pairs={{0,24},{8,16},{16,8},{24,0},{1,25},{9,17},{17,9},{25,1},{2,26},{10... | collective-permute-start | bytes 3145736 | tf_op jit(solution)/shard_map/ppermute | solution.py:24
  140.3 45.8 %collective-permute-start.1 = (bf16[256,2048]{1,0:T(8,128)(2,1)S(1)}, bf16[256,2048]{1,0:T(8,128)(2,1)S(1)}, u32[]{:S(2)}, u32[]{:S(2)}) collective-permute-start(bf16[256,2048]{1,0:T(8,128)(2,1)S(1)} %copy.180), channel_id=1, source_target_pairs={{0,16},{8,24},{16,0},{24,8},{1,17},{9,25},{17,1},{25,9},{2,18},{10... | collective-permute-start | bytes 3145736 | tf_op jit(solution)/shard_map/ppermute | solution.py:24
  140.9 45.3 %collective-permute-start = (bf16[256,2048]{1,0:T(8,128)(2,1)S(1)}, bf16[256,2048]{1,0:T(8,128)(2,1)S(1)}, u32[]{:S(2)}, u32[]{:S(2)}) collective-permute-start(bf16[256,2048]{1,0:T(8,128)(2,1)S(1)} %copy.180), channel_id=1, source_target_pairs={{0,8},{8,0},{16,24},{24,16},{1,9},{9,1},{17,25},{25,17},{2,10},{10... | collective-permute-start | bytes 3145736 | tf_op jit(solution)/shard_map/ppermute | solution.py:24
  186.8 56.9 %collective-permute-start.12 = (bf16[256,2048]{0,1:T(8,128)(2,1)S(1)}, bf16[256,2048]{0,1:T(8,128)(2,1)}, u32[]{:S(2)}, u32[]{:S(2)}) collective-permute-start(bf16[256,2048]{0,1:T(8,128)(2,1)S(1)} %bitcast.173), channel_id=1, source_target_pairs={{0,24},{8,16},{16,8},{24,0},{1,25},{9,17},{17,9},{25,1},{2,26},{10... | collective-permute-start | bytes 3145736 | tf_op jit(solution)/shard_map/ppermute | solution.py:24
  188.6 55.1 %collective-permute-start.11 = (bf16[256,2048]{0,1:T(8,128)(2,1)S(1)}, bf16[256,2048]{0,1:T(8,128)(2,1)}, u32[]{:S(2)}, u32[]{:S(2)}) collective-permute-start(bf16[256,2048]{0,1:T(8,128)(2,1)S(1)} %bitcast.174), channel_id=1, source_target_pairs={{0,16},{8,24},{16,0},{24,8},{1,17},{9,25},{17,1},{25,9},{2,18},{10... | collective-permute-start | bytes 3145736 | tf_op jit(solution)/shard_map/ppermute | solution.py:24
  189.8 53.9 %collective-permute-start.10 = (bf16[256,2048]{0,1:T(8,128)(2,1)S(1)}, bf16[256,2048]{0,1:T(8,128)(2,1)}, u32[]{:S(2)}, u32[]{:S(2)}) collective-permute-start(bf16[256,2048]{0,1:T(8,128)(2,1)S(1)} %bitcast.175), channel_id=1, source_target_pairs={{0,8},{8,0},{16,24},{24,16},{1,9},{9,1},{17,25},{25,17},{2,10},{10... | collective-permute-start | bytes 3145736 | tf_op jit(solution)/shard_map/ppermute | solution.py:24
  278.0 14.3 %collective-permute-start.13 = (bf16[4,256,1536]{2,1,0:T(8,128)(2,1)S(1)}, bf16[4,256,1536]{2,1,0:T(8,128)(2,1)}, u32[]{:S(2)}, u32[]{:S(2)}) collective-permute-start(bf16[4,256,1536]{2,1,0:T(8,128)(2,1)S(1)} %dynamic-slice_bitcast_fusion.2), channel_id=1, source_target_pairs={{0,1},{1,0},{2,3},{3,2},{4,5},{5,4},{6,7},{7,6},{8,9},{9,8},{10,11... | collective-permute-start | bytes 9437192 | tf_op jit(solution)/shard_map/ppermute | solution.py:106
  287.3 3.0 collective-permute-start.14
  298.7 219.8 %reduce-scatter.6.cloned.1.call-start = ((), (), s32[]{:S(2)}) async-start(), calls=%async_computation.12 | async-start | bytes 5242880 | tf_op jit(solution)/shard_map/reduce_scatter | solution.py:113
  341.4 17.6 %collective-permute-start.15 = (bf16[4,256,2048]{2,1,0:T(8,128)(2,1)S(1)}, bf16[4,256,2048]{2,1,0:T(8,128)(2,1)S(1)}, u32[]{:S(2)}, u32[]{:S(2)}) collective-permute-start(bf16[4,256,2048]{2,1,0:T(8,128)(2,1)S(1)} %dynamic-slice_bitcast_fusion.1), channel_id=1, source_target_pairs={{0,1},{1,0},{2,3},{3,2},{4,5},{5,4},{6,7},{7,6},{8,9},{9,8},{10,11... | collective-permute-start | bytes 12582920 | tf_op jit(solution)/shard_map/ppermute | solution.py:106
  358.6 7.5 %collective-permute-start.19 = (bf16[4,256,2048]{2,1,0:T(8,128)(2,1)}, bf16[4,256,2048]{2,1,0:T(8,128)(2,1)}, u32[]{:S(2)}, u32[]{:S(2)}) collective-permute-start(bf16[4,256,2048]{2,1,0:T(8,128)(2,1)} %dynamic-slice_bitcast_fusion), channel_id=1, source_target_pairs={{0,1},{1,0},{2,3},{3,2},{4,5},{5,4},{6,7},{7,6},{8,9},{9,8},{10,11... | collective-permute-start | bytes 12582920 | tf_op jit(solution)/shard_map/ppermute | solution.py:106
  374.0 53.0 %all-to-all-start.2 = ((bf16[4,4,64,2048]{3,2,1,0:T(8,128)(2,1)}), bf16[4,4,64,2048]{3,2,1,0:T(8,128)(2,1)}, u32[]{:S(2)}, u32[]{:S(2)}) async-start(bf16[4,4,64,2048]{3,2,1,0:T(8,128)(2,1)} %copy.207), calls=%async_computation.2 | async-start | bytes 8388608 | tf_op jit(solution)/shard_map/all_to_all | solution.py:138
  378.8 207.2 %reduce-scatter.8.cloned.1.call-start = ((), (), s32[]{:S(2)}) async-start(), calls=%async_computation.13 | async-start | bytes 5242880 | tf_op jit(solution)/shard_map/reduce_scatter | solution.py:113
  458.0 55.0 %collective-permute-start.22 = (bf16[256,2048]{1,0:T(8,128)(2,1)}, bf16[256,2048]{1,0:T(8,128)(2,1)S(1)}, u32[]{:S(2)}, u32[]{:S(2)}) collective-permute-start(bf16[256,2048]{1,0:T(8,128)(2,1)} %get-tuple-element.127), channel_id=1, source_target_pairs={{0,24},{8,16},{16,8},{24,0},{1,25},{9,17},{17,9},{25,1},{2,26},{10... | collective-permute-start | bytes 3145736 | tf_op jit(solution)/shard_map/ppermute | solution.py:24
  459.4 55.6 %collective-permute-start.21 = (bf16[256,2048]{1,0:T(8,128)(2,1)}, bf16[256,2048]{1,0:T(8,128)(2,1)S(1)}, u32[]{:S(2)}, u32[]{:S(2)}) collective-permute-start(bf16[256,2048]{1,0:T(8,128)(2,1)} %get-tuple-element.128), channel_id=1, source_target_pairs={{0,16},{8,24},{16,0},{24,8},{1,17},{9,25},{17,1},{25,9},{2,18},{10... | collective-permute-start | bytes 3145736 | tf_op jit(solution)/shard_map/ppermute | solution.py:24
  460.9 54.1 %collective-permute-start.20 = (bf16[256,2048]{1,0:T(8,128)(2,1)}, bf16[256,2048]{1,0:T(8,128)(2,1)}, u32[]{:S(2)}, u32[]{:S(2)}) collective-permute-start(bf16[256,2048]{1,0:T(8,128)(2,1)} %get-tuple-element.129), channel_id=1, source_target_pairs={{0,8},{8,0},{16,24},{24,16},{1,9},{9,1},{17,25},{25,17},{2,10},{10... | collective-permute-start | bytes 3145736 | tf_op jit(solution)/shard_map/ppermute | solution.py:24
  462.3 45.8 %all-to-all-start.3 = ((f32[32,1,256]{2,1,0:T(1,128)}), f32[32,1,256]{2,1,0:T(1,128)S(1)}, u32[]{:S(2)}, u32[]{:S(2)}) async-start(f32[32,1,256]{2,1,0:T(1,128)} %all_to_all.28), calls=%async_computation.3 | async-start | bytes 65536 | tf_op jit(solution)/shard_map/all_to_all | solution.py:296
  478.2 100.0 %collective-permute-start.18 = (bf16[256,2048]{1,0:T(8,128)(2,1)}, bf16[256,2048]{1,0:T(8,128)(2,1)}, u32[]{:S(2)}, u32[]{:S(2)}) collective-permute-start(bf16[256,2048]{1,0:T(8,128)(2,1)} %get-tuple-element.130), channel_id=1, source_target_pairs={{0,24},{8,16},{16,8},{24,0},{1,25},{9,17},{17,9},{25,1},{2,26},{10... | collective-permute-start | bytes 3145736 | tf_op jit(solution)/shard_map/ppermute | solution.py:24
  480.8 97.4 %collective-permute-start.17 = (bf16[256,2048]{1,0:T(8,128)(2,1)}, bf16[256,2048]{1,0:T(8,128)(2,1)}, u32[]{:S(2)}, u32[]{:S(2)}) collective-permute-start(bf16[256,2048]{1,0:T(8,128)(2,1)} %get-tuple-element.131), channel_id=1, source_target_pairs={{0,16},{8,24},{16,0},{24,8},{1,17},{9,25},{17,1},{25,9},{2,18},{10... | collective-permute-start | bytes 3145736 | tf_op jit(solution)/shard_map/ppermute | solution.py:24
  508.1 51.8 %all-to-all-start.4 = ((bf16[4,64,1536]{2,1,0:T(8,128)(2,1)}), bf16[4,64,1536]{2,1,0:T(8,128)(2,1)}, u32[]{:S(2)}, u32[]{:S(2)}) async-start(bf16[4,64,1536]{2,1,0:T(8,128)(2,1)} %bitcast.202), calls=%async_computation.5 | async-start | bytes 1572864 | tf_op jit(solution)/shard_map/all_to_all | solution.py:131
  513.0 65.2 %collective-permute-start.16 = (bf16[256,2048]{1,0:T(8,128)(2,1)}, bf16[256,2048]{1,0:T(8,128)(2,1)}, u32[]{:S(2)}, u32[]{:S(2)}) collective-permute-start(bf16[256,2048]{1,0:T(8,128)(2,1)} %get-tuple-element.132), channel_id=1, source_target_pairs={{0,8},{8,0},{16,24},{24,16},{1,9},{9,1},{17,25},{25,17},{2,10},{10... | collective-permute-start | bytes 3145736 | tf_op jit(solution)/shard_map/ppermute | solution.py:24
  559.9 23.4 %all-to-all-start.5 = ((bf16[4,64,2048]{2,1,0:T(8,128)(2,1)}), bf16[4,64,2048]{2,1,0:T(8,128)(2,1)}, u32[]{:S(2)}, u32[]{:S(2)}) async-start(bf16[4,64,2048]{2,1,0:T(8,128)(2,1)} %bitcast.208), calls=%async_computation.7 | async-start | bytes 2097152 | tf_op jit(solution)/shard_map/all_to_all | solution.py:131
  (45 other events, 1000.2 us)
Sparse Core Ops, SparseCore 0:
  27.7 85.0 all-gather.2
  114.4 150.0 all-gather.4
  298.8 74.6 reduce-scatter.3
  375.6 77.3 reduce-scatter.5
  455.1 77.8 reduce-scatter.7
